TPU v7x, 128 devices: a whole 4x4x4 slice. The times are simulated.
128 devices in a mesh: seq: 16 (over x, z), head: 8 (over y, core).
Axes of the slice: x: 4, y: 4, z: 4, core: 2. Of those that a mesh axis runs over, the one named last changes fastest.
Arguments:
- tokens: bfloat16 [32768, 2048], P('seq'), may hold values from -6 to 6
- norm_gain: float32 [2048], replicated, may hold values from 0.1 to 1.9
- query_weight: bfloat16 [2048, 2048], P(None, 'head'), may hold values from -0.125 to 0.125
- key_weight: bfloat16 [2048, 2048], P(None, 'head'), may hold values from -1 to 1
- value_weight: bfloat16 [2048, 2048], P(None, 'head'), may hold values from -0.125 to 0.125
- beta_weight: bfloat16 [2048, 16], P(None, 'head'), may hold values from -1 to 1
- out_gain: float32 [128], replicated, may hold values from 0.1 to 1.9
- output_weight: bfloat16 [2048, 2048], P('head'), may hold values from -0.1875 to 0.1875
- block_doc: int32 [512], P('seq'), may hold values from 0 to 3, never falling along the last dimension, each value on 1 to 192 neighbouring positions
Outputs:
- mixed: bfloat16 [32768, 2048], P('seq', 'head')
Inputs may be any that keep to these rules, and one draw needn't show every extreme that they name: `block_doc`: document numbers never fall along the window; each document covers 1 to 192 whole blocks, and one covers exactly that many.
All inputs are finite; a program needn't handle non-finite values.
Results may differ from a plain program's by a relative error of at most 0.02.
Values may be sent and summed in bfloat16 or wider, within the bound.
A program may use at most 128 MiB of HBM per device.

v0:
```python
import jax
import jax.numpy as jnp
from jax import lax
from jax.sharding import PartitionSpec as P

norm_eps = 1e-05
key_eps = 1e-06


def passed_along(block, axis, distance):
    devices = range(lax.axis_size(axis))
    route = [(i - distance, i) for i in devices if i - distance in devices]
    return lax.ppermute(block, axis, route)


def block_parts(block_q, block_k, block_v, block_b):
    highest = lax.Precision.HIGHEST
    size = block_k.shape[1]
    positions = jnp.arange(size)
    below = positions[:, None] > positions[None, :]
    causal = positions[:, None] >= positions[None, :]
    key_gram = jnp.einsum("hcd,hed->hce", block_k, block_k, precision=highest)
    unit_lower = jnp.where(below, block_b[:, :, None] * key_gram, 0.0) + jnp.eye(
        size, dtype=block_k.dtype
    )
    right_side = jnp.concatenate(
        [block_b[:, :, None] * block_k, block_b[:, :, None] * block_v], axis=2
    )
    solved = lax.linalg.triangular_solve(unit_lower, right_side, left_side=True, lower=True)
    width = block_k.shape[2]
    scores = jnp.where(causal, jnp.einsum("hcd,hed->hce", block_q, block_k, precision=highest), 0.0)
    return (solved[:, :, :width], solved[:, :, width:], scores)


def unit_norm(values):
    return values / jnp.sqrt(jnp.sum(values * values, axis=-1, keepdims=True) + key_eps)


def local(
    tokens,
    norm_gain,
    query_weight,
    key_weight,
    value_weight,
    beta_weight,
    out_gain,
    output_weight,
    block_doc,
):
    highest = lax.Precision.HIGHEST
    length = tokens.shape[0]
    local_heads = beta_weight.shape[1]
    width = query_weight.shape[1] // local_heads
    count = block_doc.shape[0]
    size = length // count
    floats = tokens.astype(jnp.float32)
    normed = (
        floats / jnp.sqrt(jnp.mean(floats * floats, axis=1, keepdims=True) + norm_eps) * norm_gain
    ).astype(jnp.bfloat16)
    queries = unit_norm(
        jax.nn.silu(jnp.dot(normed, query_weight, preferred_element_type=jnp.float32)).reshape(
            length, local_heads, width
        )
    )
    keys = unit_norm(
        jax.nn.silu(jnp.dot(normed, key_weight, preferred_element_type=jnp.float32)).reshape(
            length, local_heads, width
        )
    )
    values = jnp.dot(normed, value_weight, preferred_element_type=jnp.float32).reshape(
        length, local_heads, width
    )
    beta = jax.nn.sigmoid(jnp.dot(normed, beta_weight, preferred_element_type=jnp.float32))

    def blocked(array):
        return array.reshape(count, size, local_heads, width).transpose(0, 2, 1, 3)

    identity = jnp.broadcast_to(jnp.eye(width, dtype=jnp.float32), (local_heads, width, width))

    def advance(carry, inputs):
        state, transit, previous = carry
        block_q, block_k, block_v, block_b, doc_id = inputs
        reset = doc_id != previous
        state = jnp.where(reset, jnp.zeros_like(state), state)
        transit = jnp.where(reset, jnp.zeros_like(transit), transit)
        w_keys, u_values, scores = block_parts(block_q, block_k, block_v, block_b)
        reach = block_q - jnp.einsum("hce,hed->hcd", scores, w_keys, precision=highest)
        carried = jnp.einsum("hcd,hde->hce", reach, transit, precision=highest)
        fresh = u_values - jnp.einsum("hcd,hde->hce", w_keys, state, precision=highest)
        output = jnp.einsum("hcd,hde->hce", block_q, state, precision=highest) + jnp.einsum(
            "hce,hef->hcf", scores, fresh, precision=highest
        )
        state = state + jnp.einsum("hcd,hce->hde", block_k, fresh, precision=highest)
        moved = jnp.einsum("hcd,hde->hce", w_keys, transit, precision=highest)
        transit = transit - jnp.einsum("hcd,hce->hde", block_k, moved, precision=highest)
        return ((state, transit, doc_id), (output, carried))

    start = (jnp.zeros((local_heads, width, width), jnp.float32), identity, block_doc[0])
    inputs = (
        blocked(queries),
        blocked(keys),
        blocked(values),
        beta.reshape(count, size, local_heads).transpose(0, 2, 1),
        block_doc,
    )
    carry_end, (local_out, reach_all) = lax.scan(advance, start, inputs)
    end_state, end_transit, unused_doc = carry_end
    first_doc = block_doc[0:1].astype(jnp.float32)
    last_doc = block_doc[count - 1 : count].astype(jnp.float32)

    def relay(turn, incoming):
        sending = jnp.einsum("hde,hef->hdf", end_transit, incoming, precision=highest) + end_state
        got_state, got_last = (
            passed_along(sending.astype(jnp.bfloat16), "seq", 1).astype(sending.dtype),
            passed_along(last_doc.astype(jnp.bfloat16), "seq", 1).astype(last_doc.dtype),
        )
        return jnp.where(got_last[0] == first_doc[0], got_state, 0.0)

    incoming = lax.fori_loop(
        0, lax.axis_size("seq") - 1, relay, jnp.zeros((local_heads, width, width), jnp.float32)
    )
    heads_out = local_out + jnp.einsum("nhcd,hde->nhce", reach_all, incoming, precision=highest)
    heads_out = heads_out.transpose(0, 2, 1, 3).reshape(length, local_heads, width)
    normed_out = (
        heads_out
        / jnp.sqrt(jnp.mean(heads_out * heads_out, axis=2, keepdims=True) + norm_eps)
        * out_gain
    )
    normed_out = normed_out.reshape(length, local_heads * width).astype(jnp.bfloat16)
    partial_sum = jnp.dot(normed_out, output_weight, preferred_element_type=jnp.float32)
    mixed = lax.psum_scatter(
        partial_sum.astype(jnp.bfloat16), "head", scatter_dimension=1, tiled=True
    )
    return mixed


def solution(mesh):
    in_specs = (
        P("seq", None),
        P(),
        P(None, "head"),
        P(None, "head"),
        P(None, "head"),
        P(None, "head"),
        P(),
        P("head", None),
        P("seq"),
    )
    out_specs = P("seq", "head")
    return jax.shard_map(local, mesh=mesh, in_specs=in_specs, out_specs=out_specs, check_vma=False)
```

profile of v0, /device:TPU:1, one launch (start us, length us, event | category | flops | bytes accessed | tf_op | source)
XLA Modules:
  0.0 856.8 jit_solution(13943546094765595)
XLA Ops:
  76.3 574.4 %while.32 = (s32[]{:T(128)}, f32[2,128,128]{2,1,0:T(8,128)S(1)}, f32[2,128,128]{2,1,0:T(8,128)S(1)}, s32[]{:T(128)}, f32[32,2,64,128]{3,2,0,1:T(8,128)}, /*index...) while((s32[]{:T(128)}, f32[2,128,128]{2,1,0:T(8,128)S(1)}, ...), condition=%wide.region_4.5_spmd.clone, body=%wide.region_3.4_spmd.clone.sunk | while | flops 227024896 | bytes 3529912 | solution.py:106
  78.5 9.8 %custom-call.9 = f32[2,1,64,64]{2,3,1,0:T(8,128)S(1)} custom-call(f32[2,1,64,64]{3,2,1,0:T(8,128)S(1)} %fusion.115), custom_call_target="InvertDiagBlocksLowerTriangular" | custom-call | tf_op jit(solution)/shard_map/while/body/eval_jaxpr/triangular_solve | solution.py:29
  96.4 9.8 %custom-call.9 = f32[2,1,64,64]{2,3,1,0:T(8,128)S(1)} custom-call(f32[2,1,64,64]{3,2,1,0:T(8,128)S(1)} %fusion.115), custom_call_target="InvertDiagBlocksLowerTriangular" | custom-call | tf_op jit(solution)/shard_map/while/body/eval_jaxpr/triangular_solve | solution.py:29
  114.3 9.8 %custom-call.9 = f32[2,1,64,64]{2,3,1,0:T(8,128)S(1)} custom-call(f32[2,1,64,64]{3,2,1,0:T(8,128)S(1)} %fusion.115), custom_call_target="InvertDiagBlocksLowerTriangular" | custom-call | tf_op jit(solution)/shard_map/while/body/eval_jaxpr/triangular_solve | solution.py:29
  132.3 9.8 %custom-call.9 = f32[2,1,64,64]{2,3,1,0:T(8,128)S(1)} custom-call(f32[2,1,64,64]{3,2,1,0:T(8,128)S(1)} %fusion.115), custom_call_target="InvertDiagBlocksLowerTriangular" | custom-call | tf_op jit(solution)/shard_map/while/body/eval_jaxpr/triangular_solve | solution.py:29
  150.2 9.8 %custom-call.9 = f32[2,1,64,64]{2,3,1,0:T(8,128)S(1)} custom-call(f32[2,1,64,64]{3,2,1,0:T(8,128)S(1)} %fusion.115), custom_call_target="InvertDiagBlocksLowerTriangular" | custom-call | tf_op jit(solution)/shard_map/while/body/eval_jaxpr/triangular_solve | solution.py:29
  168.2 9.8 %custom-call.9 = f32[2,1,64,64]{2,3,1,0:T(8,128)S(1)} custom-call(f32[2,1,64,64]{3,2,1,0:T(8,128)S(1)} %fusion.115), custom_call_target="InvertDiagBlocksLowerTriangular" | custom-call | tf_op jit(solution)/shard_map/while/body/eval_jaxpr/triangular_solve | solution.py:29
  186.1 9.8 %custom-call.9 = f32[2,1,64,64]{2,3,1,0:T(8,128)S(1)} custom-call(f32[2,1,64,64]{3,2,1,0:T(8,128)S(1)} %fusion.115), custom_call_target="InvertDiagBlocksLowerTriangular" | custom-call | tf_op jit(solution)/shard_map/while/body/eval_jaxpr/triangular_solve | solution.py:29
  204.1 9.8 %custom-call.9 = f32[2,1,64,64]{2,3,1,0:T(8,128)S(1)} custom-call(f32[2,1,64,64]{3,2,1,0:T(8,128)S(1)} %fusion.115), custom_call_target="InvertDiagBlocksLowerTriangular" | custom-call | tf_op jit(solution)/shard_map/while/body/eval_jaxpr/triangular_solve | solution.py:29
  222.0 9.8 %custom-call.9 = f32[2,1,64,64]{2,3,1,0:T(8,128)S(1)} custom-call(f32[2,1,64,64]{3,2,1,0:T(8,128)S(1)} %fusion.115), custom_call_target="InvertDiagBlocksLowerTriangular" | custom-call | tf_op jit(solution)/shard_map/while/body/eval_jaxpr/triangular_solve | solution.py:29
  240.0 9.8 %custom-call.9 = f32[2,1,64,64]{2,3,1,0:T(8,128)S(1)} custom-call(f32[2,1,64,64]{3,2,1,0:T(8,128)S(1)} %fusion.115), custom_call_target="InvertDiagBlocksLowerTriangular" | custom-call | tf_op jit(solution)/shard_map/while/body/eval_jaxpr/triangular_solve | solution.py:29
  258.0 9.8 %custom-call.9 = f32[2,1,64,64]{2,3,1,0:T(8,128)S(1)} custom-call(f32[2,1,64,64]{3,2,1,0:T(8,128)S(1)} %fusion.115), custom_call_target="InvertDiagBlocksLowerTriangular" | custom-call | tf_op jit(solution)/shard_map/while/body/eval_jaxpr/triangular_solve | solution.py:29
  275.9 9.8 %custom-call.9 = f32[2,1,64,64]{2,3,1,0:T(8,128)S(1)} custom-call(f32[2,1,64,64]{3,2,1,0:T(8,128)S(1)} %fusion.115), custom_call_target="InvertDiagBlocksLowerTriangular" | custom-call | tf_op jit(solution)/shard_map/while/body/eval_jaxpr/triangular_solve | solution.py:29
  293.9 9.8 %custom-call.9 = f32[2,1,64,64]{2,3,1,0:T(8,128)S(1)} custom-call(f32[2,1,64,64]{3,2,1,0:T(8,128)S(1)} %fusion.115), custom_call_target="InvertDiagBlocksLowerTriangular" | custom-call | tf_op jit(solution)/shard_map/while/body/eval_jaxpr/triangular_solve | solution.py:29
  311.8 9.8 %custom-call.9 = f32[2,1,64,64]{2,3,1,0:T(8,128)S(1)} custom-call(f32[2,1,64,64]{3,2,1,0:T(8,128)S(1)} %fusion.115), custom_call_target="InvertDiagBlocksLowerTriangular" | custom-call | tf_op jit(solution)/shard_map/while/body/eval_jaxpr/triangular_solve | solution.py:29
  329.8 9.8 %custom-call.9 = f32[2,1,64,64]{2,3,1,0:T(8,128)S(1)} custom-call(f32[2,1,64,64]{3,2,1,0:T(8,128)S(1)} %fusion.115), custom_call_target="InvertDiagBlocksLowerTriangular" | custom-call | tf_op jit(solution)/shard_map/while/body/eval_jaxpr/triangular_solve | solution.py:29
  347.7 9.8 %custom-call.9 = f32[2,1,64,64]{2,3,1,0:T(8,128)S(1)} custom-call(f32[2,1,64,64]{3,2,1,0:T(8,128)S(1)} %fusion.115), custom_call_target="InvertDiagBlocksLowerTriangular" | custom-call | tf_op jit(solution)/shard_map/while/body/eval_jaxpr/triangular_solve | solution.py:29
  365.6 9.8 %custom-call.9 = f32[2,1,64,64]{2,3,1,0:T(8,128)S(1)} custom-call(f32[2,1,64,64]{3,2,1,0:T(8,128)S(1)} %fusion.115), custom_call_target="InvertDiagBlocksLowerTriangular" | custom-call | tf_op jit(solution)/shard_map/while/body/eval_jaxpr/triangular_solve | solution.py:29
  401.6 9.8 %custom-call.9 = f32[2,1,64,64]{2,3,1,0:T(8,128)S(1)} custom-call(f32[2,1,64,64]{3,2,1,0:T(8,128)S(1)} %fusion.115), custom_call_target="InvertDiagBlocksLowerTriangular" | custom-call | tf_op jit(solution)/shard_map/while/body/eval_jaxpr/triangular_solve | solution.py:29
  419.5 9.8 %custom-call.9 = f32[2,1,64,64]{2,3,1,0:T(8,128)S(1)} custom-call(f32[2,1,64,64]{3,2,1,0:T(8,128)S(1)} %fusion.115), custom_call_target="InvertDiagBlocksLowerTriangular" | custom-call | tf_op jit(solution)/shard_map/while/body/eval_jaxpr/triangular_solve | solution.py:29
  545.1 9.8 %custom-call.9 = f32[2,1,64,64]{2,3,1,0:T(8,128)S(1)} custom-call(f32[2,1,64,64]{3,2,1,0:T(8,128)S(1)} %fusion.115), custom_call_target="InvertDiagBlocksLowerTriangular" | custom-call | tf_op jit(solution)/shard_map/while/body/eval_jaxpr/triangular_solve | solution.py:29
  581.0 9.8 %custom-call.9 = f32[2,1,64,64]{2,3,1,0:T(8,128)S(1)} custom-call(f32[2,1,64,64]{3,2,1,0:T(8,128)S(1)} %fusion.115), custom_call_target="InvertDiagBlocksLowerTriangular" | custom-call | tf_op jit(solution)/shard_map/while/body/eval_jaxpr/triangular_solve | solution.py:29
  650.7 101.3 %while.33 = (s32[]{:T(128)}, f32[2,128,128]{2,1,0:T(8,128)S(1)}, bf16[1]{0:T(256)(128)(2,1)}, f32[1]{0:T(128)}, f32[2,128,128]{2,1,0:T(8,128)S(1)}, /*index=5*/f32[2,128,128]{2,1,0:T(8,128)S(1)}, s32[]{:T(128)}, s32[]{:T(128)}) while((s32[]{:T(128)}, f32[2,128,128]{2,1,0:T(8,128)S(1)}, bf16[1]{0:T(256)(128)(2,1)}, f32[1]{0:T(128)}, ...), condition=%wide.region_6.7_spmd.clone, body=%wide.region_5.6_spmd.clone.sunk | while | flops 50495488 | bytes 917647 | solution.py:119
  770.2 79.8 %reduce-scatter.2.cloned.1.call-done = bf16[2048,256]{1,0:T(8,128)(2,1)} async-done(((bf16[2048,2048]{1,0:T(8,128)(2,1)}), bf16[2048,256]{1,0:T(8,128)(2,1)}) %reduce-scatter.2.cloned.1.call-update) | async-done | bytes 1048592 | tf_op jit(solution)/shard_map/reduce_scatter | solution.py:131
  (671 shorter events, 501.7 us)
Async XLA Ops:
  6.5 758.0 %copy-start = (bf16[256,2048]{1,0:T(8,128)(2,1)S(1)}, bf16[256,2048]{1,0:T(8,128)(2,1)}, u32[]{:S(2)}) copy-start(bf16[256,2048]{1,0:T(8,128)(2,1)} %param.20) | copy-start | bytes 3145732
  6.5 843.4 %reduce-scatter.2.cloned.1.call-start = ((), (), s32[]{:S(2)}) async-start(), calls=%async_computation.1 | async-start | bytes 9437184 | tf_op jit(solution)/shard_map/reduce_scatter | solution.py:131
  8.5 642.2 %collective-permute-start.1 = (bf16[1]{0:T(256)(128)(2,1)}, bf16[1]{0:T(256)(128)(2,1)}, u32[]{:S(2)}, u32[]{:S(2)}) collective-permute-start(bf16[1]{0:T(256)(128)(2,1)} %convert_element_type.51), channel_id=1, source_target_pairs={{0,8},{8,16},{16,24},{24,32},{32,40},{40,48},{48,56},{56,64},{64,7... | collective-permute-start | bytes 14 | tf_op jit(solution)/shard_map/while/body/eval_jaxpr/ppermute | solution.py:13
  13.7 5.8 copy-start.2
  13.7 5.8 copy-start.4
  19.4 3.8 copy-start.7
  57.8 3.3 copy-start.5
  67.5 8.8 %copy-start.6 = (s32[32]{0:T(128)S(1)}, s32[32]{0:T(128)}, u32[]{:S(2)}) copy-start(s32[32]{0:T(128)} %param.21) | copy-start | bytes 388
  76.3 574.4 %copy-start.8 = (f32[128]{0:T(128)S(1)}, f32[128]{0:T(128)}, u32[]{:S(2)}) copy-start(f32[128]{0:T(128)} %param.19) | copy-start | bytes 1540
  651.0 4.9 collective-permute-start
  656.2 5.0 collective-permute-start
  661.5 5.0 collective-permute-start
  666.8 5.0 collective-permute-start
  672.2 5.5 collective-permute-start
  677.9 6.7 collective-permute-start
  684.9 7.0 collective-permute-start
  692.3 7.1 collective-permute-start
  699.7 7.4 collective-permute-start
  707.4 6.8 collective-permute-start
  714.5 7.5 collective-permute-start
  722.3 7.1 collective-permute-start
  729.8 7.1 collective-permute-start
  737.2 7.1 collective-permute-start
  744.6 7.4 collective-permute-start
  (2 other events, 4.9 us)
Sparse Core Ops, SparseCore 0:
  770.3 79.5 reduce-scatter.1
where the time goes:
time: 861 us; the launch traced here: 857 us
  other arithmetic  363 us (42%)
  matrix products  172 us (20%)
  waiting for transfers between devices  92.5 us (11%)
  starting transfers between devices  80.5 us (9%)
  local copies, waits for them, and re-layouts  79.7 us (9%)
  loops' own time  53.9 us (6%)
  between operations  14.9 us (2%)
    another operation x32, other arithmetic, block_parts(): lax.linalg.triangular_solve(unit_lower, right_side, left_side=True, lower...  315 us
    ppermute x16, starting transfers between devices, passed_along(): return lax.ppermute(block, axis, route)  80.5 us
    reduce_scatter x1, waiting for transfers between devices, local(): lax.psum_scatter(partial_sum.astype(jnp.bfloat16), 'head', scatter_dimens...  79.8 us
    dynamic_slice x64, local copies, waits for them, and re-layouts, local(): carry_end, (local_out, reach_all) = lax.scan(advance, start, inputs)  49.4 us
    another operation x1, loops' own time, local(): carry_end, (local_out, reach_all) = lax.scan(advance, start, inputs)  44.9 us
    mul x32, other arithmetic, block_parts(): block_b[:, :, None] * block_k  29.6 us
    dot_general x32, matrix products, advance(): carried = jnp.einsum('hcd,hde->hce', reach, transit, precision=highest)  27.8 us
    dot_general x32, matrix products, advance(): jnp.einsum('hce,hef->hcf', scores, fresh, precision=highest)  26.3 us
  transfers between devices with their start and end apart: 17, of which 16 were waited for; matrix products, arithmetic and copies ran while one was open for 69% of the time, Pallas kernels for 0%

commit v1 on v0

v1 whole, which is shorter than its diff:
```python
import jax
import jax.numpy as jnp
from jax import lax
from jax.experimental import pallas as pl
from jax.experimental.pallas import tpu as pltpu
from jax.sharding import PartitionSpec as P

norm_eps = 1e-05
key_eps = 1e-06
BLOCK = 64
MOST_BLOCKS = 192
DK = 128
STEP = 256
f32 = jnp.float32
bf16 = jnp.bfloat16
LEVELS = (2, 4, 8, 16, 32, 64)


def dot(a, b):
    return jnp.dot(a, b, preferred_element_type=f32)


def dot_nt(a, b):
    return lax.dot_general(a, b, (((1,), (1,)), ((), ())), preferred_element_type=f32)


def dot_tn(a, b):
    return lax.dot_general(a, b, (((0,), (0,)), ((), ())), preferred_element_type=f32)


def unit(values):
    act = values * jax.nn.sigmoid(values)
    return act * lax.rsqrt(jnp.sum(act * act, axis=1, keepdims=True) + key_eps)


def fill_masks(strict, causal, pair, off):
    shape = (STEP, STEP)
    row = lax.broadcasted_iota(jnp.int32, shape, 0)
    col = lax.broadcasted_iota(jnp.int32, shape, 1)
    same = (row // DK) == (col // DK)
    strict[...] = jnp.where(same & (row > col), 1.0, 0.0).astype(f32)
    causal[...] = jnp.where(same & (row >= col), 1.0, 0.0).astype(f32)
    pair[...] = jnp.where((row // 2 == col // 2) & (row > col), 1.0, 0.0).astype(f32)
    for n, s in enumerate(LEVELS):
        hit = (row // (2 * s) == col // (2 * s)) & (row // s > col // s)
        off[n] = jnp.where(hit, 1.0, 0.0).astype(bf16)


def delta_step(kf, vf, qb, beta, doc, i, ps, masks):
    strict, causal, pair, off = masks
    d = [doc[4 * i + j] for j in range(4)]
    before = doc[jnp.maximum(4 * i - 1, 0)]
    link = [
        jnp.where((before == d[0]) | (i == 0), 1.0, 0.0).astype(f32),
        jnp.where(d[1] == d[2], 1.0, 0.0).astype(f32),
    ]
    join = [
        jnp.where(d[0] == d[1], 1.0, 0.0).astype(f32),
        jnp.where(d[2] == d[3], 1.0, 0.0).astype(f32),
    ]
    row = lax.broadcasted_iota(jnp.int32, (STEP, 1), 0)
    second = (row % DK) >= BLOCK
    chunk1 = row >= DK
    join_r = jnp.where(chunk1, join[1], join[0])
    link_r = jnp.where(chunk1, link[1], link[0])
    enters = jnp.where(second, link_r * join_r, link_r)
    leaves = jnp.where(second, 1.0, join_r)
    col = lax.broadcasted_iota(jnp.int32, (1, STEP), 1)
    cross = jnp.where(second, join_r, 1.0)
    col_first = (col % DK) < BLOCK
    kb = kf.astype(bf16)
    doc_mask = jnp.where(col_first, cross, 1.0)
    a = dot_nt(kb, kb) * beta * (strict[...] * doc_mask)
    scores = dot_nt(qb, kb) * (causal[...] * doc_mask)
    a_hi = a.astype(bf16)
    a_lo = (a - a_hi.astype(f32)).astype(bf16)
    eye = causal[...] - strict[...]
    x = eye - a * pair[...]
    for n in range(len(LEVELS)):
        xb = x.astype(bf16)
        x = x - dot(xb, dot(a_hi * off[n], xb).astype(bf16))
    xb = x.astype(bf16)
    kr = kb.astype(f32)
    right = jnp.concatenate([beta * enters * kr, beta * vf], axis=1)
    y = dot(xb, right.astype(bf16)).astype(bf16)
    left = right - y.astype(f32) - dot(a_hi, y) - dot(a_lo, y)
    wu = (y.astype(f32) + dot(xb, left.astype(bf16))).astype(bf16)
    mixed = dot(scores.astype(bf16), wu)
    reach = (enters * qb.astype(f32) - mixed[:, :DK]).astype(bf16)
    k_end = (kr * leaves).astype(bf16)
    outs, carried = [], []
    for c in range(2):
        rows = slice(c * DK, (c + 1) * DK)
        step = dot_tn(k_end[rows], wu[rows])
        state = ps[...]
        sb = state.astype(bf16)
        seen = dot(reach[rows], sb)
        carried.append(seen[:, :DK])
        outs.append(mixed[rows, DK:] + seen[:, DK:])
        moved = dot(step[:, :DK].astype(bf16), sb)
        keep = link[c] * join[c]
        gain = jnp.concatenate([jnp.zeros((DK, DK), f32), step[:, DK:]], axis=1)
        ps[...] = keep * state - moved + gain
    return jnp.concatenate(outs, axis=0), jnp.concatenate(carried, axis=0)


def local_kernel(
    doc, tok, gain, wq, wk, wv, wb, out, carried, ps_out,
    weights, normed, later_q, beta_all, ps, strict, causal, pair, off, sems,
):
    h, i = pl.program_id(0), pl.program_id(1)
    rows = pl.ds(pl.multiple_of(i * STEP, STEP), STEP)
    masks = (strict, causal, pair, off)

    @pl.when((h == 0) & (i == 0))
    def _():
        copies = []
        for n, (source, column) in enumerate(
            [(wk, 0), (wv, 0), (wk, 1), (wv, 1), (wq, 0), (wq, 1)]
        ):
            copies.append(
                pltpu.make_async_copy(
                    source.at[:, column * DK : (column + 1) * DK],
                    weights.at[:, n * DK : (n + 1) * DK],
                    sems.at[n],
                )
            )
        for copy in copies:
            copy.start()
        fill_masks(*masks)
        weights[:, 6 * DK :] = jnp.concatenate(
            [wb[...], jnp.zeros((wb.shape[0], DK - wb.shape[1]), bf16)], axis=1
        )
        for copy in copies:
            copy.wait()

    @pl.when(i == 0)
    def _():
        row = lax.broadcasted_iota(jnp.int32, (DK, 2 * DK), 0)
        col = lax.broadcasted_iota(jnp.int32, (DK, 2 * DK), 1)
        ps[...] = jnp.where(row == col, 1.0, 0.0).astype(f32)

    @pl.when(h == 0)
    def _():
        floats = tok[...].astype(f32)
        scale = lax.rsqrt(jnp.mean(floats * floats, axis=1, keepdims=True) + norm_eps)
        n = (floats * scale * gain[...]).astype(bf16)
        normed[rows, :] = n
        rest = dot(n, weights[:, 4 * DK :])
        q0 = unit(rest[:, :DK]).astype(bf16)
        later_q[0, rows, :] = q0
        later_q[1, rows, :] = unit(rest[:, DK : 2 * DK]).astype(bf16)
        beta_all[rows, :] = jax.nn.sigmoid(rest[:, 2 * DK :])

    kv = dot(normed[rows, :], weights[:, pl.ds(pl.multiple_of(h * 2 * DK, 2 * DK), 2 * DK)])
    kf = unit(kv[:, :DK])
    both = beta_all[rows, :]
    beta = jnp.where(h == 0, both[:, 0:1], both[:, 1:2])
    o, c = delta_step(kf, kv[:, DK:], later_q[h, rows, :], beta, doc, i, ps, masks)
    out[0] = o
    carried[0] = c.astype(bf16)

    @pl.when(i == pl.num_programs(1) - 1)
    def _():
        ps_out[0] = ps[...]


def local_pass(doc, tokens, gain, wq, wk, wv, wb):
    length, width = tokens.shape
    heads = wb.shape[1]
    steps = length // STEP
    any_spec = pl.BlockSpec(memory_space=pl.ANY)
    return pl.pallas_call(
        local_kernel,
        grid_spec=pltpu.PrefetchScalarGridSpec(
            num_scalar_prefetch=1,
            grid=(heads, steps),
            in_specs=[
                pl.BlockSpec((STEP, width), lambda h, i, doc: (jnp.where(h == 0, i, steps - 1), 0)),
                pl.BlockSpec((1, width), lambda h, i, doc: (0, 0)),
                any_spec,
                any_spec,
                any_spec,
                pl.BlockSpec(wb.shape, lambda h, i, doc: (0, 0)),
            ],
            out_specs=[
                pl.BlockSpec((1, STEP, DK), lambda h, i, doc: (h, i, 0)),
                pl.BlockSpec((1, STEP, DK), lambda h, i, doc: (h, i, 0)),
                pl.BlockSpec((1, DK, 2 * DK), lambda h, i, doc: (h, 0, 0)),
            ],
            scratch_shapes=[
                pltpu.VMEM((width, 7 * DK), bf16),
                pltpu.VMEM((length, width), bf16),
                pltpu.VMEM((heads, length, DK), bf16),
                pltpu.VMEM((length, DK), f32),
                pltpu.VMEM((DK, 2 * DK), f32),
                pltpu.VMEM((STEP, STEP), f32),
                pltpu.VMEM((STEP, STEP), f32),
                pltpu.VMEM((STEP, STEP), f32),
                pltpu.VMEM((len(LEVELS), STEP, STEP), bf16),
                pltpu.SemaphoreType.DMA((6,)),
            ],
        ),
        out_shape=[
            jax.ShapeDtypeStruct((heads, length, DK), f32),
            jax.ShapeDtypeStruct((heads, length, DK), bf16),
            jax.ShapeDtypeStruct((heads, DK, 2 * DK), f32),
        ],
        compiler_params=pltpu.CompilerParams(vmem_limit_bytes=48 << 20),
        name="local_pass",
    )(doc, tokens, gain, wq, wk, wv, wb)


def output_kernel(out, carried, incoming, gain, weight, partial):
    columns = []
    for h in range(out.shape[0]):
        o = out[h] + dot(carried[h], incoming[h])
        scale = lax.rsqrt(jnp.mean(o * o, axis=1, keepdims=True) + norm_eps)
        columns.append((o * scale * gain[...]).astype(bf16))
    partial[...] = dot(jnp.concatenate(columns, axis=1), weight[...]).astype(bf16)


def output_pass(out, carried, incoming, gain, weight):
    heads, length, _ = out.shape
    return pl.pallas_call(
        output_kernel,
        grid=(length // STEP,),
        in_specs=[
            pl.BlockSpec((heads, STEP, DK), lambda i: (0, i, 0)),
            pl.BlockSpec((heads, STEP, DK), lambda i: (0, i, 0)),
            pl.BlockSpec(incoming.shape, lambda i: (0, 0, 0)),
            pl.BlockSpec((1, DK), lambda i: (0, 0)),
            pl.BlockSpec(weight.shape, lambda i: (0, 0)),
        ],
        out_specs=pl.BlockSpec((STEP, weight.shape[1]), lambda i: (i, 0)),
        out_shape=jax.ShapeDtypeStruct((length, weight.shape[1]), bf16),
        compiler_params=pltpu.CompilerParams(vmem_limit_bytes=32 << 20),
        name="output_pass",
    )(out, carried, incoming, gain, weight)


def passed_along(block, axis):
    route = [(i, i + 1) for i in range(lax.axis_size(axis) - 1)]
    return lax.ppermute(block, axis, route)


def local(tokens, norm_gain, wq, wk, wv, wb, out_gain, wo, block_doc):
    count = block_doc.shape[0]
    out, carried, ps = local_pass(block_doc, tokens, norm_gain[None, :], wq, wk, wv, wb)
    transit, state = ps[:, :, :DK], ps[:, :, DK:]
    first = block_doc[0:1].astype(f32)
    last = block_doc[count - 1 : count].astype(bf16)
    before = passed_along(last, "seq").astype(f32)
    follows = (before[0] == first[0]) & (lax.axis_index("seq") > 0)
    incoming = jnp.zeros_like(state)
    for turn in range(MOST_BLOCKS // count):
        end = state if turn == 0 else jnp.einsum("hde,hef->hdf", transit, incoming) + state
        got = passed_along(end.astype(bf16), "seq").astype(f32)
        incoming = jnp.where(follows, got, 0.0)
    partial = output_pass(out, carried, incoming.astype(bf16), out_gain[None, :], wo)
    return lax.psum_scatter(partial, "head", scatter_dimension=1, tiled=True)


def solution(mesh):
    in_specs = (
        P("seq", None),
        P(),
        P(None, "head"),
        P(None, "head"),
        P(None, "head"),
        P(None, "head"),
        P(),
        P("head", None),
        P("seq"),
    )
    return jax.shard_map(
        local, mesh=mesh, in_specs=in_specs, out_specs=P("seq", "head"), check_vma=False
    )
```

time: 861 us -> 216 us (0.25)
  other arithmetic: 363 us -> 0.02 us
  matrix products: 172 us -> 0.75 us
  Pallas kernels: 0 us -> 84.5 us
  local copies, waits for them, and re-layouts: 79.7 us -> 11.5 us
  loops' own time: 53.9 us -> 0 us
  starting transfers between devices: 80.5 us -> 27.9 us
  waiting for transfers between devices: 92.5 us -> 76.7 us
    another operation x34 -> x1, other arithmetic: 315 us -> 0.01 us  [the longest x32 315 us: block_parts(): lax.linalg.triangular_solve(unit_lower, right_side, left_side=True, lower...]
    dot_general x341 -> x5, matrix products: 162 us -> 0.75 us  [local(): jnp.einsum('hde,hef->hdf', transit, incoming) + state]
    pallas_call x0 -> x2, Pallas kernels: none -> 84.5 us  [the longest x1 79 us: local_pass(): pl.pallas_call(local_kernel, grid_spec=pltpu.PrefetchScalarGridSpec(num_s...]
    another operation x2 -> x0, loops' own time: 53.9 us -> none  [the longest x1 44.9 us: local(): carry_end, (local_out, reach_all) = lax.scan(advance, start, inputs)]
    ppermute x16 -> x7, starting transfers between devices: 80.5 us -> 27.9 us  [passed_along(): return lax.ppermute(block, axis, route)]
    dynamic_slice x64 -> x0, local copies, waits for them, and re-layouts: 49.4 us -> none  [local(): carry_end, (local_out, reach_all) = lax.scan(advance, start, inputs)]
    mul x32 -> x0, other arithmetic: 29.6 us -> none  [block_parts(): block_b[:, :, None] * block_k]
    reduce_scatter x1, waiting for transfers between devices: 79.8 us -> 68.9 us  [local(): return lax.psum_scatter(partial, 'head', scatter_dimension=1, tiled=True)]
  transfers between devices with their start and end apart: 17 -> 8, of which waited for: 16 -> 7; matrix products, arithmetic and copies ran while one was open for 69% -> 0% of each run, Pallas kernels for 0% -> 0%
where the time goes in v1:
time: 216 us
  Pallas kernels  84.5 us (39%)
  waiting for transfers between devices  76.7 us (36%)
  starting transfers between devices  27.9 us (13%)
  between operations  14.2 us (7%)
  local copies, waits for them, and re-layouts  11.5 us (5%)
    pallas_call x1, Pallas kernels, local_pass(): pl.pallas_call(local_kernel, grid_spec=pltpu.PrefetchScalarGridSpec(num_s...  79 us
    reduce_scatter x1, waiting for transfers between devices, local(): return lax.psum_scatter(partial, 'head', scatter_dimension=1, tiled=True)  68.9 us
    ppermute x7, starting transfers between devices, passed_along(): return lax.ppermute(block, axis, route)  27.9 us
    unnamed x21, local copies, waits for them, and re-layouts  10.9 us
    ppermute x7, waiting for transfers between devices, passed_along(): return lax.ppermute(block, axis, route)  7.78 us
    pallas_call x1, Pallas kernels, output_pass(): pl.pallas_call(output_kernel, grid=(length // STEP,), in_specs=[pl.BlockS...  5.48 us
  transfers between devices with their start and end apart: 8, of which 7 were waited for; matrix products, arithmetic and copies ran while one was open for 0% of the time, Pallas kernels for 0%

profile of v1, /device:TPU:1, one launch (start us, length us, event | category | flops | bytes accessed | tf_op | source)
XLA Modules:
  0.0 215.6 jit_solution(10403905314825381159)
XLA Ops:
  6.5 1.1 copy.10.wb
  7.6 1.2 copy-done.3
  8.9 1.2 copy-done.4
  10.1 1.2 copy-done.5
  11.3 0.7 copy-done.6
  12.0 0.7 copy-done.8
  12.7 79.0 %local_pass.1 = (f32[2,2048,128]{2,1,0:T(8,128)}, bf16[2,2048,128]{2,1,0:T(8,128)(2,1)S(1)}, f32[2,128,256]{2,1,0:T(8,128)S(1)}) custom-call(s32[32]{0:T(128)S(1)} %copy-done.8, bf16[2048,2048]{1,0:T(8,128)(2,1)} %tok.1, f32[1,2048]{1,0:T(1,128)S(1)} %bitcast.4, bf16[2048,256]{1,0:T(8,128)(2,1)S(1)} %copy-done.3, bf16[2048,256]{1,0:T(8,128)(2,1)S(1)} %copy-done.4, ...), custom_call_target="tpu_custom_call" | custom-call | tf_op jit(solution)/shard_map/local_pass/pallas_call | solution.py:173
  91.7 4.4 %collective-permute-start.1 = (bf16[2,128,128]{2,1,0:T(8,128)(2,1)S(1)}, bf16[2,128,128]{2,1,0:T(8,128)(2,1)S(1)}, u32[]{:S(2)}, u32[]{:S(2)}) collective-permute-start(bf16[2,128,128]{2,1,0:T(8,128)(2,1)S(1)} %slice.33), channel_id=1, source_target_pairs={{0,8},{8,16},{16,24},{24,32},{32,40},{40,48},{48,56},{56,64},{64,7... | collective-permute-start | bytes 196616 | tf_op jit(solution)/shard_map/ppermute | solution.py:244
  96.1 0.6 slice.13
  96.7 4.0 %collective-permute-start = (bf16[1]{0:T(256)(128)(2,1)}, bf16[1]{0:T(256)(128)(2,1)}, u32[]{:S(2)}, u32[]{:S(2)}) collective-permute-start(bf16[1]{0:T(256)(128)(2,1)} %slice.13), channel_id=1, source_target_pairs={{0,8},{8,16},{16,24},{24,32},{32,40},{40,48},{48,56},{56,64},{64,7... | collective-permute-start | bytes 14 | tf_op jit(solution)/shard_map/ppermute | solution.py:244
  101.8 3.5 %collective-permute-start.2 = (bf16[2,128,128]{2,1,0:T(8,128)(2,1)S(1)}, bf16[2,128,128]{2,1,0:T(8,128)(2,1)S(1)}, u32[]{:S(2)}, u32[]{:S(2)}) collective-permute-start(bf16[2,128,128]{2,1,0:T(8,128)(2,1)S(1)} %fusion), channel_id=1, source_target_pairs={{0,8},{8,16},{16,24},{24,32},{32,40},{40,48},{48,56},{56,64},{64,7... | collective-permute-start | bytes 196616 | tf_op jit(solution)/shard_map/ppermute | solution.py:244
  105.3 1.3 collective-permute-done.2
  106.8 3.7 %collective-permute-start.3 = (bf16[2,128,128]{2,1,0:T(8,128)(2,1)S(1)}, bf16[2,128,128]{2,1,0:T(8,128)(2,1)S(1)}, u32[]{:S(2)}, u32[]{:S(2)}) collective-permute-start(bf16[2,128,128]{2,1,0:T(8,128)(2,1)S(1)} %fusion.1), channel_id=1, source_target_pairs={{0,8},{8,16},{16,24},{24,32},{32,40},{40,48},{48,56},{56,64},{64,7... | collective-permute-start | bytes 196616 | tf_op jit(solution)/shard_map/ppermute | solution.py:244
  110.5 1.3 collective-permute-done.3
  112.0 3.7 %collective-permute-start.4 = (bf16[2,128,128]{2,1,0:T(8,128)(2,1)S(1)}, bf16[2,128,128]{2,1,0:T(8,128)(2,1)S(1)}, u32[]{:S(2)}, u32[]{:S(2)}) collective-permute-start(bf16[2,128,128]{2,1,0:T(8,128)(2,1)S(1)} %fusion.2), channel_id=1, source_target_pairs={{0,8},{8,16},{16,24},{24,32},{32,40},{40,48},{48,56},{56,64},{64,7... | collective-permute-start | bytes 196616 | tf_op jit(solution)/shard_map/ppermute | solution.py:244
  115.7 1.3 collective-permute-done.4
  117.1 3.7 %collective-permute-start.5 = (bf16[2,128,128]{2,1,0:T(8,128)(2,1)S(1)}, bf16[2,128,128]{2,1,0:T(8,128)(2,1)S(1)}, u32[]{:S(2)}, u32[]{:S(2)}) collective-permute-start(bf16[2,128,128]{2,1,0:T(8,128)(2,1)S(1)} %fusion.3), channel_id=1, source_target_pairs={{0,8},{8,16},{16,24},{24,32},{32,40},{40,48},{48,56},{56,64},{64,7... | collective-permute-start | bytes 196616 | tf_op jit(solution)/shard_map/ppermute | solution.py:244
  120.8 1.8 collective-permute-done.5
  122.7 4.9 %collective-permute-start.6 = (bf16[2,128,128]{2,1,0:T(8,128)(2,1)S(1)}, bf16[2,128,128]{2,1,0:T(8,128)(2,1)S(1)}, u32[]{:S(2)}, u32[]{:S(2)}) collective-permute-start(bf16[2,128,128]{2,1,0:T(8,128)(2,1)S(1)} %fusion.4), channel_id=1, source_target_pairs={{0,8},{8,16},{16,24},{24,32},{32,40},{40,48},{48,56},{56,64},{64,7... | collective-permute-start | bytes 196616 | tf_op jit(solution)/shard_map/ppermute | solution.py:244
  127.7 1.8 collective-permute-done.6
  129.5 1.6 copy-done.1
  131.1 5.5 %output_pass.1 = bf16[2048,2048]{1,0:T(8,128)(2,1)S(1)} custom-call(f32[2,2048,128]{2,1,0:T(8,128)S(1)} %copy-done.1, bf16[2,2048,128]{2,1,0:T(8,128)(2,1)S(1)} %get-tuple-element.9.carried, bf16[2,128,128]{2,1,0:T(8,128)(2,1)S(1)} %select_convert_fusion.incoming, f32[1,128]{1,0:T(1,128)S(1)} %bitcast.5, bf16[256,2048]{1,0:T(8,128)(2,1)S(1)} %copy-done.2), custom_call_target="tpu_custom_call" | custom-call | tf_op jit(solution)/shard_map/output_pass/pallas_call | solution.py:225
  136.6 3.2 %copy-done = bf16[2048,2048]{1,0:T(8,128)(2,1)} copy-done((bf16[2048,2048]{1,0:T(8,128)(2,1)}, bf16[2048,2048]{1,0:T(8,128)(2,1)S(1)}, u32[]{:S(2)}) %copy-start) | copy-done | bytes 8388632
  139.8 68.9 %reduce-scatter.2.cloned.1.call-done = bf16[2048,256]{1,0:T(8,128)(2,1)} async-done(((bf16[2048,2048]{1,0:T(8,128)(2,1)}), bf16[2048,256]{1,0:T(8,128)(2,1)}) %reduce-scatter.2.cloned.1.call-update) | async-done | bytes 1048592 | tf_op jit(solution)/shard_map/reduce_scatter | solution.py:261
  (25 shorter events, 1.1 us)
Async XLA Ops:
  6.5 122.9 %copy-start.2 = (bf16[256,2048]{1,0:T(8,128)(2,1)S(1)}, bf16[256,2048]{1,0:T(8,128)(2,1)}, u32[]{:S(2)}) copy-start(bf16[256,2048]{1,0:T(8,128)(2,1)} %weight.1) | copy-start | bytes 3145732
  6.5 202.2 %reduce-scatter.2.cloned.1.call-start = ((), (), s32[]{:S(2)}) async-start(), calls=%async_computation.1 | async-start | bytes 9437184 | tf_op jit(solution)/shard_map/reduce_scatter | solution.py:261
  7.6 1.2 copy-start.3
  8.9 1.2 copy-start.4
  10.1 1.2 copy-start.5
  11.3 0.7 copy-start.6
  12.0 0.7 copy-start.8
  12.7 88.0 %copy-start.9 = (s32[32]{0:T(128)S(1)}, s32[32]{0:T(128)}, u32[]{:S(2)}) copy-start(s32[32]{0:T(128)} %doc.1) | copy-start | bytes 388
  12.7 116.8 %copy-start.7 = (f32[128]{0:T(128)S(1)}, f32[128]{0:T(128)}, u32[]{:S(2)}) copy-start(f32[128]{0:T(128)} %param.15) | copy-start | bytes 1540
  91.7 9.9 %collective-permute-start.1 = (bf16[2,128,128]{2,1,0:T(8,128)(2,1)S(1)}, bf16[2,128,128]{2,1,0:T(8,128)(2,1)S(1)}, u32[]{:S(2)}, u32[]{:S(2)}) collective-permute-start(bf16[2,128,128]{2,1,0:T(8,128)(2,1)S(1)} %slice.33), channel_id=1, source_target_pairs={{0,8},{8,16},{16,24},{24,32},{32,40},{40,48},{48,56},{56,64},{64,7... | collective-permute-start | bytes 196616 | tf_op jit(solution)/shard_map/ppermute | solution.py:244
  96.7 4.4 %collective-permute-start = (bf16[1]{0:T(256)(128)(2,1)}, bf16[1]{0:T(256)(128)(2,1)}, u32[]{:S(2)}, u32[]{:S(2)}) collective-permute-start(bf16[1]{0:T(256)(128)(2,1)} %slice.13), channel_id=1, source_target_pairs={{0,8},{8,16},{16,24},{24,32},{32,40},{40,48},{48,56},{56,64},{64,7... | collective-permute-start | bytes 14 | tf_op jit(solution)/shard_map/ppermute | solution.py:244
  101.8 4.8 %collective-permute-start.2 = (bf16[2,128,128]{2,1,0:T(8,128)(2,1)S(1)}, bf16[2,128,128]{2,1,0:T(8,128)(2,1)S(1)}, u32[]{:S(2)}, u32[]{:S(2)}) collective-permute-start(bf16[2,128,128]{2,1,0:T(8,128)(2,1)S(1)} %fusion), channel_id=1, source_target_pairs={{0,8},{8,16},{16,24},{24,32},{32,40},{40,48},{48,56},{56,64},{64,7... | collective-permute-start | bytes 196616 | tf_op jit(solution)/shard_map/ppermute | solution.py:244
  106.8 5.0 %collective-permute-start.3 = (bf16[2,128,128]{2,1,0:T(8,128)(2,1)S(1)}, bf16[2,128,128]{2,1,0:T(8,128)(2,1)S(1)}, u32[]{:S(2)}, u32[]{:S(2)}) collective-permute-start(bf16[2,128,128]{2,1,0:T(8,128)(2,1)S(1)} %fusion.1), channel_id=1, source_target_pairs={{0,8},{8,16},{16,24},{24,32},{32,40},{40,48},{48,56},{56,64},{64,7... | collective-permute-start | bytes 196616 | tf_op jit(solution)/shard_map/ppermute | solution.py:244
  112.0 5.0 %collective-permute-start.4 = (bf16[2,128,128]{2,1,0:T(8,128)(2,1)S(1)}, bf16[2,128,128]{2,1,0:T(8,128)(2,1)S(1)}, u32[]{:S(2)}, u32[]{:S(2)}) collective-permute-start(bf16[2,128,128]{2,1,0:T(8,128)(2,1)S(1)} %fusion.2), channel_id=1, source_target_pairs={{0,8},{8,16},{16,24},{24,32},{32,40},{40,48},{48,56},{56,64},{64,7... | collective-permute-start | bytes 196616 | tf_op jit(solution)/shard_map/ppermute | solution.py:244
  117.1 5.5 %collective-permute-start.5 = (bf16[2,128,128]{2,1,0:T(8,128)(2,1)S(1)}, bf16[2,128,128]{2,1,0:T(8,128)(2,1)S(1)}, u32[]{:S(2)}, u32[]{:S(2)}) collective-permute-start(bf16[2,128,128]{2,1,0:T(8,128)(2,1)S(1)} %fusion.3), channel_id=1, source_target_pairs={{0,8},{8,16},{16,24},{24,32},{32,40},{40,48},{48,56},{56,64},{64,7... | collective-permute-start | bytes 196616 | tf_op jit(solution)/shard_map/ppermute | solution.py:244
  122.7 6.7 %collective-permute-start.6 = (bf16[2,128,128]{2,1,0:T(8,128)(2,1)S(1)}, bf16[2,128,128]{2,1,0:T(8,128)(2,1)S(1)}, u32[]{:S(2)}, u32[]{:S(2)}) collective-permute-start(bf16[2,128,128]{2,1,0:T(8,128)(2,1)S(1)} %fusion.4), channel_id=1, source_target_pairs={{0,8},{8,16},{16,24},{24,32},{32,40},{40,48},{48,56},{56,64},{64,7... | collective-permute-start | bytes 196616 | tf_op jit(solution)/shard_map/ppermute | solution.py:244
  129.5 1.6 copy-start.1
  136.6 3.2 %copy-start = (bf16[2048,2048]{1,0:T(8,128)(2,1)}, bf16[2048,2048]{1,0:T(8,128)(2,1)S(1)}, u32[]{:S(2)}) copy-start(bf16[2048,2048]{1,0:T(8,128)(2,1)S(1)} %output_pass.1) | copy-start | bytes 25165828
Sparse Core Ops, SparseCore 0:
  140.0 68.7 reduce-scatter.1

commit v2 on v1

v2 whole, which is shorter than its diff:
```python
import jax
import jax.numpy as jnp
from jax import lax
from jax.experimental import pallas as pl
from jax.experimental.pallas import tpu as pltpu
from jax.sharding import PartitionSpec as P

norm_eps = 1e-05
key_eps = 1e-06
BLOCK = 64
MOST_BLOCKS = 192
DK = 128
STEP = 256
TILE = 512
f32 = jnp.float32
bf16 = jnp.bfloat16
LEVELS = (2, 4, 8, 16, 32, 64)


def dot(a, b):
    return jnp.dot(a, b, preferred_element_type=f32)


def dot_nt(a, b):
    return lax.dot_general(a, b, (((1,), (1,)), ((), ())), preferred_element_type=f32)


def dot_tn(a, b):
    return lax.dot_general(a, b, (((0,), (0,)), ((), ())), preferred_element_type=f32)


def unit(values):
    act = values * jax.nn.sigmoid(values)
    return act * lax.rsqrt(jnp.sum(act * act, axis=1, keepdims=True) + key_eps)


def fill_masks(strict, causal, pair, off):
    shape = (STEP, STEP)
    row = lax.broadcasted_iota(jnp.int32, shape, 0)
    col = lax.broadcasted_iota(jnp.int32, shape, 1)
    same = (row // DK) == (col // DK)
    strict[...] = jnp.where(same & (row > col), 1.0, 0.0).astype(f32)
    if causal is not None:
        causal[...] = jnp.where(same & (row >= col), 1.0, 0.0).astype(f32)
    pair[0] = jnp.where((row // 2 == col // 2) & (row > col), 1.0, 0.0).astype(bf16)
    pair[1] = jnp.where(row == col, 1.0, 0.0).astype(bf16)
    for n, s in enumerate(LEVELS):
        hit = (row // (2 * s) == col // (2 * s)) & (row // s > col // s)
        off[n] = jnp.where(hit, 1.0, 0.0).astype(bf16)


def scaled_weight(weight, gain):
    column = jnp.transpose(jnp.broadcast_to(gain[...], (DK, gain.shape[1])))
    parts = [
        weight[:, n * DK : (n + 1) * DK].astype(f32) * column for n in range(weight.shape[1] // DK)
    ]
    return jnp.concatenate(parts, axis=1).astype(bf16)


def doc_masks(doc, at):
    d = [doc[at + j] for j in range(4)]
    before = doc[jnp.maximum(at - 1, 0)]
    link = [
        jnp.where((before == d[0]) | (at == 0), 1.0, 0.0).astype(f32),
        jnp.where(d[1] == d[2], 1.0, 0.0).astype(f32),
    ]
    join = [
        jnp.where(d[0] == d[1], 1.0, 0.0).astype(f32),
        jnp.where(d[2] == d[3], 1.0, 0.0).astype(f32),
    ]
    row = lax.broadcasted_iota(jnp.int32, (STEP, 1), 0)
    second = (row % DK) >= BLOCK
    join_r = jnp.where(row >= DK, join[1], join[0])
    link_r = jnp.where(row >= DK, link[1], link[0])
    enters = jnp.where(second, link_r * join_r, link_r)
    leaves = jnp.where(second, 1.0, join_r)
    cross = jnp.where(second, join_r, 1.0)
    col = lax.broadcasted_iota(jnp.int32, (1, STEP), 1)
    full = jnp.where((col % DK) < BLOCK, cross, 1.0)
    return enters, leaves, full, [link[c] * join[c] for c in range(2)]


def interleave(main, side, every):
    count = 0
    for _ in main:
        count += 1
        if count % every == 0:
            next(side, None)
    for _ in side:
        pass


def project_keys(x, scale_out, weights, kbuf, vbuf, bbuf, slot):
    halves = x.shape[0] // STEP
    scales = []
    for m in range(halves):
        rows = slice(m * STEP, (m + 1) * STEP)
        floats = x[rows, :].astype(f32)
        r = lax.rsqrt(jnp.mean(floats * floats, axis=1, keepdims=True) + norm_eps)
        scales.append(r)
        scale_out[rows, :] = jnp.broadcast_to(r, (STEP, DK))
        yield
        b = dot(x[rows, :], weights[:, 4 * DK :]) * r
        bbuf[slot, rows, :] = jax.nn.sigmoid(b)
        yield
        for h in range(2):
            kv = dot(x[rows, :], weights[:, 2 * h * DK : 2 * (h + 1) * DK]) * r
            kbuf[slot, h, rows, :] = unit(kv[:, :DK]).astype(bf16)
            vbuf[slot, h, rows, :] = kv[:, DK:]
            yield


def solve_keys(doc, at, kbuf, vbuf, bbuf, slot, ps, masks, wu_out, ps_all):
    strict, pair, off, wu_buf, end_buf = masks
    halves = kbuf.shape[2] // STEP
    groups = [(h, g) for g in range(halves) for h in range(2)]
    dm = [doc_masks(doc, at + 4 * g) for g in range(halves)]
    keys, a_hi, a_lo, xb, t, right, y, wu = {}, {}, {}, {}, {}, {}, {}, {}
    beta = {}
    for h, g in groups:
        rows = slice(g * STEP, (g + 1) * STEP)
        keys[h, g] = kbuf[slot, h, rows, :]
        beta[h, g] = bbuf[slot, rows, h : h + 1]
        a = dot_nt(keys[h, g], keys[h, g]) * beta[h, g] * (strict[...] * dm[g][2])
        hi = a.astype(bf16)
        a_hi[h, g] = hi
        a_lo[h, g] = (a - hi.astype(f32)).astype(bf16)
        xb[h, g] = pair[1] - hi * pair[0]
        yield
    for n in range(len(LEVELS)):
        for at_group in groups:
            t[at_group] = dot(a_hi[at_group] * off[n], xb[at_group]).astype(bf16)
        yield
        for at_group in groups:
            xb[at_group] = xb[at_group] - dot(xb[at_group], t[at_group]).astype(bf16)
        yield
    for h, g in groups:
        rows = slice(g * STEP, (g + 1) * STEP)
        b = beta[h, g]
        right[h, g] = jnp.concatenate(
            [(b * dm[g][0]) * keys[h, g].astype(f32), b * vbuf[slot, h, rows, :]], axis=1
        )
        y[h, g] = dot(xb[h, g], right[h, g].astype(bf16)).astype(bf16)
    yield
    left = {}
    for k in groups:
        rest = right[k] - y[k].astype(f32) - dot(a_hi[k], y[k]) - dot(a_lo[k], y[k])
        left[k] = rest.astype(bf16)
    yield
    for h, g in groups:
        wu[h, g] = (y[h, g].astype(f32) + dot(xb[h, g], left[h, g])).astype(bf16)
        wu_out[h, g * STEP : (g + 1) * STEP, :] = wu[h, g]
    yield
    step = {}
    for h, g in groups:
        k_end = (keys[h, g].astype(f32) * dm[g][1]).astype(bf16)
        for c in range(2):
            rows = slice(c * DK, (c + 1) * DK)
            step[h, g, c] = dot_tn(k_end[rows], wu[h, g][rows])
    yield
    for g in range(halves):
        for c in range(2):
            for h in range(2):
                state = ps[h]
                sb = state.astype(bf16)
                ps_all[h, 2 * g + c] = sb
                move = step[h, g, c]
                moved = dot(move[:, :DK].astype(bf16), sb)
                gain = jnp.concatenate([jnp.zeros((DK, DK), f32), move[:, DK:]], axis=1)
                ps[h] = dm[g][3][c] * state - moved + gain
            yield


def keys_kernel(
    doc, x, gain, wk, wv, wb, k_out, wu_out, ps_all, ps_end, scale_out,
    weights, kbuf, vbuf, bbuf, ps, strict, pair, off,
):
    i, last = pl.program_id(0), pl.num_programs(0) - 1
    tile = x.shape[0]
    blocks = tile // BLOCK

    def project():
        return project_keys(x, scale_out, weights, kbuf, vbuf, bbuf, i % 2)

    def solve():
        slot = (i + 1) % 2
        k_out[...] = kbuf[slot]
        return solve_keys(
            doc, (i - 1) * blocks, kbuf, vbuf, bbuf, slot, ps,
            (strict, pair, off, None, None), wu_out, ps_all,
        )

    @pl.when(i == 0)
    def _():
        fill_masks(strict, None, pair, off)
        sk, sv = scaled_weight(wk, gain), scaled_weight(wv, gain)
        for h in range(2):
            weights[:, 2 * h * DK : (2 * h + 1) * DK] = sk[:, h * DK : (h + 1) * DK]
            weights[:, (2 * h + 1) * DK : (2 * h + 2) * DK] = sv[:, h * DK : (h + 1) * DK]
        wide = jnp.concatenate(
            [wb[...], jnp.zeros((wb.shape[0], DK - wb.shape[1]), bf16)], axis=1
        )
        weights[:, 4 * DK :] = scaled_weight(wide, gain)
        row = lax.broadcasted_iota(jnp.int32, (DK, 2 * DK), 0)
        col = lax.broadcasted_iota(jnp.int32, (DK, 2 * DK), 1)
        for h in range(2):
            ps[h] = jnp.where(row == col, 1.0, 0.0).astype(f32)
        for _ in project():
            pass

    @pl.when((i > 0) & (i < last))
    def _():
        interleave(solve(), project(), 2)

    @pl.when(i == last)
    def _():
        for _ in solve():
            pass
        for h in range(2):
            ps_end[h] = ps[h].astype(bf16)


def keys_pass(doc, tokens, gain, wk, wv, wb):
    length, width = tokens.shape
    heads = wb.shape[1]
    steps = length // TILE
    chunks = TILE // DK
    after = lambda i: jnp.maximum(i - 1, 0)
    whole = lambda shape: pl.BlockSpec(shape, lambda i, doc: (0,) * len(shape))
    return pl.pallas_call(
        keys_kernel,
        grid_spec=pltpu.PrefetchScalarGridSpec(
            num_scalar_prefetch=1,
            grid=(steps + 1,),
            in_specs=[
                pl.BlockSpec((TILE, width), lambda i, doc: (jnp.minimum(i, steps - 1), 0)),
                whole((1, width)),
                whole(wk.shape),
                whole(wv.shape),
                whole(wb.shape),
            ],
            out_specs=[
                pl.BlockSpec((heads, TILE, DK), lambda i, doc: (0, after(i), 0)),
                pl.BlockSpec((heads, TILE, 2 * DK), lambda i, doc: (0, after(i), 0)),
                pl.BlockSpec((heads, chunks, DK, 2 * DK), lambda i, doc: (0, after(i), 0, 0)),
                whole((heads, DK, 2 * DK)),
                pl.BlockSpec((TILE, DK), lambda i, doc: (jnp.minimum(i, steps - 1), 0)),
            ],
            scratch_shapes=[
                pltpu.VMEM((width, 5 * DK), bf16),
                pltpu.VMEM((2, heads, TILE, DK), bf16),
                pltpu.VMEM((2, heads, TILE, DK), f32),
                pltpu.VMEM((2, TILE, DK), f32),
                pltpu.VMEM((heads, DK, 2 * DK), f32),
                pltpu.VMEM((STEP, STEP), f32),
                pltpu.VMEM((2, STEP, STEP), bf16),
                pltpu.VMEM((len(LEVELS), STEP, STEP), bf16),
            ],
        ),
        out_shape=[
            jax.ShapeDtypeStruct((heads, length, DK), bf16),
            jax.ShapeDtypeStruct((heads, length, 2 * DK), bf16),
            jax.ShapeDtypeStruct((heads, length // DK, DK, 2 * DK), bf16),
            jax.ShapeDtypeStruct((heads, DK, 2 * DK), bf16),
            jax.ShapeDtypeStruct((length, DK), f32),
        ],
        compiler_params=pltpu.CompilerParams(vmem_limit_bytes=56 << 20),
        cost_estimate=pl.CostEstimate(
            flops=2 * length * width * 5 * DK, bytes_accessed=20 << 20, transcendentals=0
        ),
        name="keys_pass",
    )(doc, tokens, gain, wk, wv, wb)


def query_tile(doc, at, x, scale, weights, keys, wu, ps_all, causal, out, carried):
    groups = [(h, g) for g in range(x.shape[0] // STEP) for h in range(2)]
    dm = [doc_masks(doc, at + 4 * g) for g in range(x.shape[0] // STEP)]
    qb, mixed, scores = {}, {}, {}
    for g in range(x.shape[0] // STEP):
        rows = slice(g * STEP, (g + 1) * STEP)
        both = dot(x[rows, :], weights[...]) * scale[rows, 0:1]
        for h in range(2):
            qb[h, g] = unit(both[:, h * DK : (h + 1) * DK]).astype(bf16)
    for h, g in groups:
        rows = slice(g * STEP, (g + 1) * STEP)
        s = dot_nt(qb[h, g], keys[h, rows, :]) * (causal[...] * dm[g][2])
        scores[h, g] = s.astype(bf16)
    for h, g in groups:
        rows = slice(g * STEP, (g + 1) * STEP)
        mixed[h, g] = dot(scores[h, g], wu[h, rows, :])
    for h, g in groups:
        reach = (dm[g][0] * qb[h, g].astype(f32) - mixed[h, g][:, :DK]).astype(bf16)
        for c in range(2):
            rows = slice(c * DK, (c + 1) * DK)
            to = slice(g * STEP + c * DK, g * STEP + (c + 1) * DK)
            seen = dot(reach[rows], ps_all[h, 2 * g + c])
            carried[h, to, :] = seen[:, :DK].astype(bf16)
            out[h, to, :] = mixed[h, g][rows, DK:] + seen[:, DK:]


def query_kernel(doc, x, gain, scale, wq, keys, wu, ps_all, out, carried, weights, causal):
    i = pl.program_id(0)

    @pl.when(i == 0)
    def _():
        weights[...] = scaled_weight(wq, gain)
        row = lax.broadcasted_iota(jnp.int32, (STEP, STEP), 0)
        col = lax.broadcasted_iota(jnp.int32, (STEP, STEP), 1)
        same = (row // DK) == (col // DK)
        causal[...] = jnp.where(same & (row >= col), 1.0, 0.0).astype(f32)

    query_tile(
        doc, i * (x.shape[0] // BLOCK), x, scale, weights, keys, wu, ps_all, causal, out, carried
    )


def query_pass(doc, tokens, gain, scale, wq, keys, wu, ps_all):
    length, width = tokens.shape
    heads = keys.shape[0]
    steps = length // TILE
    whole = lambda shape: pl.BlockSpec(shape, lambda i, doc: (0,) * len(shape))
    part = lambda *tail: pl.BlockSpec((heads, TILE) + tail, lambda i, doc: (0, i) + (0,) * len(tail))
    return pl.pallas_call(
        query_kernel,
        grid_spec=pltpu.PrefetchScalarGridSpec(
            num_scalar_prefetch=1,
            grid=(steps,),
            in_specs=[
                pl.BlockSpec((TILE, width), lambda i, doc: (i, 0)),
                whole((1, width)),
                pl.BlockSpec((TILE, DK), lambda i, doc: (i, 0)),
                whole(wq.shape),
                part(DK),
                part(2 * DK),
                pl.BlockSpec(
                    (heads, TILE // DK, DK, 2 * DK), lambda i, doc: (0, i, 0, 0)
                ),
            ],
            out_specs=[part(DK), part(DK)],
            scratch_shapes=[pltpu.VMEM(wq.shape, bf16), pltpu.VMEM((STEP, STEP), f32)],
        ),
        out_shape=[
            jax.ShapeDtypeStruct((heads, length, DK), f32),
            jax.ShapeDtypeStruct((heads, length, DK), bf16),
        ],
        compiler_params=pltpu.CompilerParams(vmem_limit_bytes=56 << 20),
        cost_estimate=pl.CostEstimate(
            flops=2 * length * width * 3 * DK, bytes_accessed=14 << 20, transcendentals=0
        ),
        name="query_pass",
    )(doc, tokens, gain, scale, wq, keys, wu, ps_all)


def output_kernel(out, carried, incoming, gain, weight, partial):
    columns = []
    for h in range(out.shape[0]):
        o = out[h] + dot(carried[h], incoming[h])
        scale = lax.rsqrt(jnp.mean(o * o, axis=1, keepdims=True) + norm_eps)
        columns.append((o * scale * gain[...]).astype(bf16))
    partial[...] = dot(jnp.concatenate(columns, axis=1), weight[...]).astype(bf16)


def output_pass(out, carried, incoming, gain, weight):
    heads, length, _ = out.shape
    return pl.pallas_call(
        output_kernel,
        grid=(length // STEP,),
        in_specs=[
            pl.BlockSpec((heads, STEP, DK), lambda i: (0, i, 0)),
            pl.BlockSpec((heads, STEP, DK), lambda i: (0, i, 0)),
            pl.BlockSpec(incoming.shape, lambda i: (0, 0, 0)),
            pl.BlockSpec((1, DK), lambda i: (0, 0)),
            pl.BlockSpec(weight.shape, lambda i: (0, 0)),
        ],
        out_specs=pl.BlockSpec((STEP, weight.shape[1]), lambda i: (i, 0)),
        out_shape=jax.ShapeDtypeStruct((length, weight.shape[1]), bf16),
        compiler_params=pltpu.CompilerParams(vmem_limit_bytes=32 << 20),
        name="output_pass",
    )(out, carried, incoming, gain, weight)


def passed_along(block, axis):
    route = [(i, i + 1) for i in range(lax.axis_size(axis) - 1)]
    return lax.ppermute(block, axis, route)


def local(tokens, norm_gain, wq, wk, wv, wb, out_gain, wo, block_doc):
    count = block_doc.shape[0]
    gain = norm_gain[None, :]
    keys, wu, ps_all, ps, scale = keys_pass(block_doc, tokens, gain, wk, wv, wb)
    out, carried = query_pass(block_doc, tokens, gain, scale, wq, keys, wu, ps_all)
    transit, state = ps[:, :, :DK].astype(f32), ps[:, :, DK:].astype(f32)
    first = block_doc[0:1].astype(f32)
    last = block_doc[count - 1 : count].astype(bf16)
    before = passed_along(last, "seq").astype(f32)
    follows = (before[0] == first[0]) & (lax.axis_index("seq") > 0)
    incoming = jnp.zeros_like(state)
    for turn in range(MOST_BLOCKS // count):
        end = state if turn == 0 else jnp.einsum("hde,hef->hdf", transit, incoming) + state
        got = passed_along(end.astype(bf16), "seq").astype(f32)
        incoming = jnp.where(follows, got, 0.0)
    partial = output_pass(out, carried, incoming.astype(bf16), out_gain[None, :], wo)
    return lax.psum_scatter(partial, "head", scatter_dimension=1, tiled=True)


def solution(mesh):
    in_specs = (
        P("seq", None),
        P(),
        P(None, "head"),
        P(None, "head"),
        P(None, "head"),
        P(None, "head"),
        P(),
        P("head", None),
        P("seq"),
    )
    return jax.shard_map(
        local, mesh=mesh, in_specs=in_specs, out_specs=P("seq", "head"), check_vma=False
    )
```

time: 216 us -> 177 us (0.82)
  Pallas kernels: 84.5 us -> 46.2 us
  matrix products: 0.75 us -> 5.11 us
  waiting for transfers between devices: 76.7 us -> 73.1 us
  local copies, waits for them, and re-layouts: 11.5 us -> 9.3 us
    pallas_call x1 -> x2, Pallas kernels: 79 us -> 40.8 us  [the longest x1 29.7 us: keys_pass(): pl.pallas_call(keys_kernel, grid_spec=pltpu.PrefetchScalarGridSpec(num_sc...]
    dot_general x5, matrix products: 0.75 us -> 5.11 us  [local(): jnp.einsum('hde,hef->hdf', transit, incoming) + state]
    unnamed x21 -> x13, local copies, waits for them, and re-layouts: 10.9 us -> 7.79 us
    ppermute x7, waiting for transfers between devices: 7.78 us -> 5.61 us  [passed_along(): return lax.ppermute(block, axis, route)]
  transfers between devices with their start and end apart: 8 -> 8, of which waited for: 7 -> 6; matrix products, arithmetic and copies ran while one was open for 0% -> 0% of each run, Pallas kernels for 0% -> 6%
where the time goes in v2:
time: 177 us
  waiting for transfers between devices  73.1 us (41%)
  Pallas kernels  46.2 us (26%)
  starting transfers between devices  28.6 us (16%)
  between operations  14.2 us (8%)
  local copies, waits for them, and re-layouts  9.3 us (5%)
  matrix products  5.11 us (3%)
    reduce_scatter x1, waiting for transfers between devices, local(): return lax.psum_scatter(partial, 'head', scatter_dimension=1, tiled=True)  67.5 us
    pallas_call x1, Pallas kernels, keys_pass(): pl.pallas_call(keys_kernel, grid_spec=pltpu.PrefetchScalarGridSpec(num_sc...  29.7 us
    ppermute x7, starting transfers between devices, passed_along(): return lax.ppermute(block, axis, route)  28.6 us
    pallas_call x1, Pallas kernels, query_pass(): pl.pallas_call(query_kernel, grid_spec=pltpu.PrefetchScalarGridSpec(num_s...  11.1 us
    unnamed x13, local copies, waits for them, and re-layouts  7.79 us
    ppermute x7, waiting for transfers between devices, passed_along(): return lax.ppermute(block, axis, route)  5.61 us
    pallas_call x1, Pallas kernels, output_pass(): pl.pallas_call(output_kernel, grid=(length // STEP,), in_specs=[pl.BlockS...  5.49 us
    dot_general x5, matrix products, local(): jnp.einsum('hde,hef->hdf', transit, incoming) + state  5.11 us
  transfers between devices with their start and end apart: 8, of which 6 were waited for; matrix products, arithmetic and copies ran while one was open for 0% of the time, Pallas kernels for 6%

profile of v2, /device:TPU:1, one launch (start us, length us, event | category | flops | bytes accessed | tf_op | source)
XLA Modules:
  0.0 176.6 jit_solution(6978381001713422698)
XLA Ops:
  6.5 1.8 copy.10.wb
  8.3 29.7 %keys_pass.1 = (bf16[2,2048,128]{2,1,0:T(8,128)(2,1)}, bf16[2,2048,256]{2,1,0:T(8,128)(2,1)}, bf16[2,16,128,256]{3,2,1,0:T(8,128)(2,1)}, bf16[2,128,256]{2,1,0:T(8,128)(2,1)}, f32[2048,128]{1,0:T(8,128)}) custom-call(s32[32]{0:T(128)} %doc.3, bf16[2048,2048]{1,0:T(8,128)(2,1)} %x.3, f32[1,2048]{1,0:T(1,128)} %bitcast.5, bf16[2048,256]{1,0:T(8,128)(2,1)} %wk.1, ...), custom_call_target="tpu_custom_call" | custom-call | flops 5368709120 | bytes 20971520 | tf_op jit(solution)/shard_map/keys_pass/pallas_call | solution.py:230
  38.8 4.5 %collective-permute-start.1 = (bf16[2,128,128]{2,1,0:T(8,128)(2,1)S(1)}, bf16[2,128,128]{2,1,0:T(8,128)(2,1)S(1)}, u32[]{:S(2)}, u32[]{:S(2)}) collective-permute-start(bf16[2,128,128]{2,1,0:T(8,128)(2,1)S(1)} %slice.16), channel_id=1, source_target_pairs={{0,8},{8,16},{16,24},{24,32},{32,40},{40,48},{48,56},{56,64},{64,7... | collective-permute-start | bytes 196616 | tf_op jit(solution)/shard_map/ppermute | solution.py:384
  44.1 4.0 %collective-permute-start = (bf16[1]{0:T(256)(128)(2,1)}, bf16[1]{0:T(256)(128)(2,1)}, u32[]{:S(2)}, u32[]{:S(2)}) collective-permute-start(bf16[1]{0:T(256)(128)(2,1)} %slice.13), channel_id=1, source_target_pairs={{0,8},{8,16},{16,24},{24,32},{32,40},{40,48},{48,56},{56,64},{64,7... | collective-permute-start | bytes 14 | tf_op jit(solution)/shard_map/ppermute | solution.py:384
  49.1 1.0 fusion
  50.1 3.5 %collective-permute-start.2 = (bf16[2,128,128]{2,1,0:T(8,128)(2,1)S(1)}, bf16[2,128,128]{2,1,0:T(8,128)(2,1)S(1)}, u32[]{:S(2)}, u32[]{:S(2)}) collective-permute-start(bf16[2,128,128]{2,1,0:T(8,128)(2,1)S(1)} %fusion), channel_id=1, source_target_pairs={{0,8},{8,16},{16,24},{24,32},{32,40},{40,48},{48,56},{56,64},{64,7... | collective-permute-start | bytes 196616 | tf_op jit(solution)/shard_map/ppermute | solution.py:384
  53.7 1.3 collective-permute-done.2
  55.0 1.0 fusion.1
  56.0 3.7 %collective-permute-start.3 = (bf16[2,128,128]{2,1,0:T(8,128)(2,1)S(1)}, bf16[2,128,128]{2,1,0:T(8,128)(2,1)S(1)}, u32[]{:S(2)}, u32[]{:S(2)}) collective-permute-start(bf16[2,128,128]{2,1,0:T(8,128)(2,1)S(1)} %fusion.1), channel_id=1, source_target_pairs={{0,8},{8,16},{16,24},{24,32},{32,40},{40,48},{48,56},{56,64},{64,7... | collective-permute-start | bytes 196616 | tf_op jit(solution)/shard_map/ppermute | solution.py:384
  59.7 1.3 collective-permute-done.3
  61.0 1.0 fusion.2
  62.0 3.7 %collective-permute-start.4 = (bf16[2,128,128]{2,1,0:T(8,128)(2,1)S(1)}, bf16[2,128,128]{2,1,0:T(8,128)(2,1)S(1)}, u32[]{:S(2)}, u32[]{:S(2)}) collective-permute-start(bf16[2,128,128]{2,1,0:T(8,128)(2,1)S(1)} %fusion.2), channel_id=1, source_target_pairs={{0,8},{8,16},{16,24},{24,32},{32,40},{40,48},{48,56},{56,64},{64,7... | collective-permute-start | bytes 196616 | tf_op jit(solution)/shard_map/ppermute | solution.py:384
  65.7 1.3 collective-permute-done.4
  67.0 1.0 fusion.3
  68.1 3.7 %collective-permute-start.5 = (bf16[2,128,128]{2,1,0:T(8,128)(2,1)S(1)}, bf16[2,128,128]{2,1,0:T(8,128)(2,1)S(1)}, u32[]{:S(2)}, u32[]{:S(2)}) collective-permute-start(bf16[2,128,128]{2,1,0:T(8,128)(2,1)S(1)} %fusion.3), channel_id=1, source_target_pairs={{0,8},{8,16},{16,24},{24,32},{32,40},{40,48},{48,56},{56,64},{64,7... | collective-permute-start | bytes 196616 | tf_op jit(solution)/shard_map/ppermute | solution.py:384
  71.8 1.3 collective-permute-done.5
  73.1 1.0 fusion.4
  74.1 5.4 %collective-permute-start.6 = (bf16[2,128,128]{2,1,0:T(8,128)(2,1)S(1)}, bf16[2,128,128]{2,1,0:T(8,128)(2,1)S(1)}, u32[]{:S(2)}, u32[]{:S(2)}) collective-permute-start(bf16[2,128,128]{2,1,0:T(8,128)(2,1)S(1)} %fusion.4), channel_id=1, source_target_pairs={{0,8},{8,16},{16,24},{24,32},{32,40},{40,48},{48,56},{56,64},{64,7... | collective-permute-start | bytes 196616 | tf_op jit(solution)/shard_map/ppermute | solution.py:384
  79.6 11.1 %query_pass.1 = (f32[2,2048,128]{2,1,0:T(8,128)}, bf16[2,2048,128]{2,1,0:T(8,128)(2,1)}) custom-call(s32[32]{0:T(128)} %doc.3, bf16[2048,2048]{1,0:T(8,128)(2,1)} %x.3, f32[1,2048]{1,0:T(1,128)} %bitcast.6, f32[2048,128]{1,0:T(8,128)} %get-tuple-element.12.scale, bf16[2048,256]{1,0:T(8,128)(2,1)} %wq.1, bf16[2,2048,128]{2,1,0:T(8,128)(2,1)} %get-tuple-element.13.keys, ...), custom_call_target="tpu_custom_call" | custom-call | flops 3221225472 | bytes 14680064 | tf_op jit(solution)/shard_map/query_pass/pallas_call | solution.py:323
  90.7 1.6 copy-done.1
  92.3 1.2 copy-done.3
  93.5 5.5 %output_pass.1 = bf16[2048,2048]{1,0:T(8,128)(2,1)S(1)} custom-call(f32[2,2048,128]{2,1,0:T(8,128)S(1)} %copy-done.1, bf16[2,2048,128]{2,1,0:T(8,128)(2,1)S(1)} %copy-done.3, bf16[2,128,128]{2,1,0:T(8,128)(2,1)S(1)} %select_convert_fusion.incoming, f32[1,128]{1,0:T(1,128)S(1)} %bitcast.4, bf16[256,2048]{1,0:T(8,128)(2,1)S(1)} %copy-done.2), custom_call_target="tpu_custom_call" | custom-call | tf_op jit(solution)/shard_map/output_pass/pallas_call | solution.py:365
  99.0 3.2 %copy-done = bf16[2048,2048]{1,0:T(8,128)(2,1)} copy-done((bf16[2048,2048]{1,0:T(8,128)(2,1)}, bf16[2048,2048]{1,0:T(8,128)(2,1)S(1)}, u32[]{:S(2)}) %copy-start) | copy-done | bytes 8388632
  102.2 67.5 %reduce-scatter.2.cloned.1.call-done = bf16[2048,256]{1,0:T(8,128)(2,1)} async-done(((bf16[2048,2048]{1,0:T(8,128)(2,1)}), bf16[2048,256]{1,0:T(8,128)(2,1)}) %reduce-scatter.2.cloned.1.call-update) | async-done | bytes 1048592 | tf_op jit(solution)/shard_map/reduce_scatter | solution.py:403
  (18 shorter events, 1.9 us)
Async XLA Ops:
  6.5 163.2 %reduce-scatter.2.cloned.1.call-start = ((), (), s32[]{:S(2)}) async-start(), calls=%async_computation.1 | async-start | bytes 9437184 | tf_op jit(solution)/shard_map/reduce_scatter | solution.py:403
  8.3 35.1 %copy-start.5 = (s32[32]{0:T(128)S(1)}, s32[32]{0:T(128)}, u32[]{:S(2)}) copy-start(s32[32]{0:T(128)} %doc.3) | copy-start | bytes 388
  38.8 10.3 %collective-permute-start.1 = (bf16[2,128,128]{2,1,0:T(8,128)(2,1)S(1)}, bf16[2,128,128]{2,1,0:T(8,128)(2,1)S(1)}, u32[]{:S(2)}, u32[]{:S(2)}) collective-permute-start(bf16[2,128,128]{2,1,0:T(8,128)(2,1)S(1)} %slice.16), channel_id=1, source_target_pairs={{0,8},{8,16},{16,24},{24,32},{32,40},{40,48},{48,56},{56,64},{64,7... | collective-permute-start | bytes 196616 | tf_op jit(solution)/shard_map/ppermute | solution.py:384
  44.1 4.5 %collective-permute-start = (bf16[1]{0:T(256)(128)(2,1)}, bf16[1]{0:T(256)(128)(2,1)}, u32[]{:S(2)}, u32[]{:S(2)}) collective-permute-start(bf16[1]{0:T(256)(128)(2,1)} %slice.13), channel_id=1, source_target_pairs={{0,8},{8,16},{16,24},{24,32},{32,40},{40,48},{48,56},{56,64},{64,7... | collective-permute-start | bytes 14 | tf_op jit(solution)/shard_map/ppermute | solution.py:384
  50.1 4.8 %collective-permute-start.2 = (bf16[2,128,128]{2,1,0:T(8,128)(2,1)S(1)}, bf16[2,128,128]{2,1,0:T(8,128)(2,1)S(1)}, u32[]{:S(2)}, u32[]{:S(2)}) collective-permute-start(bf16[2,128,128]{2,1,0:T(8,128)(2,1)S(1)} %fusion), channel_id=1, source_target_pairs={{0,8},{8,16},{16,24},{24,32},{32,40},{40,48},{48,56},{56,64},{64,7... | collective-permute-start | bytes 196616 | tf_op jit(solution)/shard_map/ppermute | solution.py:384
  56.0 5.0 %collective-permute-start.3 = (bf16[2,128,128]{2,1,0:T(8,128)(2,1)S(1)}, bf16[2,128,128]{2,1,0:T(8,128)(2,1)S(1)}, u32[]{:S(2)}, u32[]{:S(2)}) collective-permute-start(bf16[2,128,128]{2,1,0:T(8,128)(2,1)S(1)} %fusion.1), channel_id=1, source_target_pairs={{0,8},{8,16},{16,24},{24,32},{32,40},{40,48},{48,56},{56,64},{64,7... | collective-permute-start | bytes 196616 | tf_op jit(solution)/shard_map/ppermute | solution.py:384
  62.0 5.0 %collective-permute-start.4 = (bf16[2,128,128]{2,1,0:T(8,128)(2,1)S(1)}, bf16[2,128,128]{2,1,0:T(8,128)(2,1)S(1)}, u32[]{:S(2)}, u32[]{:S(2)}) collective-permute-start(bf16[2,128,128]{2,1,0:T(8,128)(2,1)S(1)} %fusion.2), channel_id=1, source_target_pairs={{0,8},{8,16},{16,24},{24,32},{32,40},{40,48},{48,56},{56,64},{64,7... | collective-permute-start | bytes 196616 | tf_op jit(solution)/shard_map/ppermute | solution.py:384
  68.1 5.0 %collective-permute-start.5 = (bf16[2,128,128]{2,1,0:T(8,128)(2,1)S(1)}, bf16[2,128,128]{2,1,0:T(8,128)(2,1)S(1)}, u32[]{:S(2)}, u32[]{:S(2)}) collective-permute-start(bf16[2,128,128]{2,1,0:T(8,128)(2,1)S(1)} %fusion.3), channel_id=1, source_target_pairs={{0,8},{8,16},{16,24},{24,32},{32,40},{40,48},{48,56},{56,64},{64,7... | collective-permute-start | bytes 196616 | tf_op jit(solution)/shard_map/ppermute | solution.py:384
  74.1 16.5 %collective-permute-start.6 = (bf16[2,128,128]{2,1,0:T(8,128)(2,1)S(1)}, bf16[2,128,128]{2,1,0:T(8,128)(2,1)S(1)}, u32[]{:S(2)}, u32[]{:S(2)}) collective-permute-start(bf16[2,128,128]{2,1,0:T(8,128)(2,1)S(1)} %fusion.4), channel_id=1, source_target_pairs={{0,8},{8,16},{16,24},{24,32},{32,40},{40,48},{48,56},{56,64},{64,7... | collective-permute-start | bytes 196616 | tf_op jit(solution)/shard_map/ppermute | solution.py:384
  79.5 11.1 %copy-start.2 = (bf16[256,2048]{1,0:T(8,128)(2,1)S(1)}, bf16[256,2048]{1,0:T(8,128)(2,1)}, u32[]{:S(2)}) copy-start(bf16[256,2048]{1,0:T(8,128)(2,1)} %weight.1) | copy-start | bytes 3145732
  79.6 11.1 %copy-start.4 = (f32[128]{0:T(128)S(1)}, f32[128]{0:T(128)}, u32[]{:S(2)}) copy-start(f32[128]{0:T(128)} %param.15) | copy-start | bytes 1540
  90.7 1.6 copy-start.1
  92.3 1.2 copy-start.3
  99.0 3.2 %copy-start = (bf16[2048,2048]{1,0:T(8,128)(2,1)}, bf16[2048,2048]{1,0:T(8,128)(2,1)S(1)}, u32[]{:S(2)}) copy-start(bf16[2048,2048]{1,0:T(8,128)(2,1)S(1)} %output_pass.1) | copy-start | bytes 25165828
Sparse Core Ops, SparseCore 0:
  102.4 67.3 reduce-scatter.1

commit v3 on v2

--- a/solution.py
+++ b/solution.py
@@ -8,7 +8,6 @@
 norm_eps = 1e-05
 key_eps = 1e-06
 BLOCK = 64
-MOST_BLOCKS = 192
 DK = 128
 STEP = 256
 TILE = 512
@@ -298,28 +297,106 @@
             out[h, to, :] = mixed[h, g][rows, DK:] + seen[:, DK:]
 
 
-def query_kernel(doc, x, gain, scale, wq, keys, wu, ps_all, out, carried, weights, causal):
-    i = pl.program_id(0)
+def peer(s, h):
+    return dict(device_id=(s, h), device_id_type=pl.DeviceIdType.MESH)
+
+
+def join(first, then, follows):
+    moved = jnp.where(follows, dot(then[:, :DK], first), 0.0)
+    gain = jnp.concatenate([jnp.zeros((DK, DK), f32), then[:, DK:].astype(f32)], axis=1)
+    return (moved + gain).astype(bf16)
+
+
+def query_kernel(
+    doc, x, gain, scale, wq, keys, wu, ps_all, ps, out_gain, result,
+    weights, causal, out, carried, own, near, three, far1, far4, send, recv,
+):
+    i, last = pl.program_id(0), pl.num_programs(0) - 1
+    tile = x.shape[0]
+    heads = keys.shape[0]
+    count = result.shape[0] // BLOCK
+    s, h = lax.axis_index("seq"), lax.axis_index("head")
+    n = lax.axis_size("seq")
+    to = lambda d: peer(lax.rem(s + d + n, n), h)
+    foot = heads * DK
+
+    def move(src, dst, at, d):
+        return pltpu.make_async_remote_copy(
+            src_ref=src, dst_ref=dst, send_sem=send.at[at], recv_sem=recv.at[at], **to(d)
+        )
+
+    first_copies = [move(own, near.at[0], 0, 1), move(own, near.at[1], 1, 2)]
+    second_copies = [
+        move(three, far1, 2, 1),
+        move(three.at[:, DK:], far4, 3, 4),
+    ]
 
     @pl.when(i == 0)
     def _():
+        barrier = pltpu.get_barrier_semaphore()
+        for d in (1, -1, 2, -2, 4, -4):
+            pl.semaphore_signal(barrier, inc=1, **to(d))
+        for k in range(heads):
+            own[k * DK : (k + 1) * DK, :] = ps[k]
+        own[foot:, :DK] = jnp.full((16, DK), doc[0].astype(f32)).astype(bf16)
+        own[foot:, DK:] = jnp.full((16, DK), doc[count - 1].astype(f32)).astype(bf16)
+        pl.semaphore_wait(barrier, 6)
+        for copy in first_copies:
+            copy.start()
         weights[...] = scaled_weight(wq, gain)
         row = lax.broadcasted_iota(jnp.int32, (STEP, STEP), 0)
         col = lax.broadcasted_iota(jnp.int32, (STEP, STEP), 1)
         same = (row // DK) == (col // DK)
         causal[...] = jnp.where(same & (row >= col), 1.0, 0.0).astype(f32)
 
+    @pl.when(i == last)
+    def _():
+        for copy in first_copies:
+            copy.wait()
+        first_own, last_before = own[foot : foot + 1, 0:1], near[0, foot : foot + 1, DK : DK + 1]
+        first_before, last_two = near[0, foot : foot + 1, 0:1], near[1, foot : foot + 1, DK : DK + 1]
+        for k in range(heads):
+            rows = slice(k * DK, (k + 1) * DK)
+            two = join(near[1, rows, :], near[0, rows, :], (last_two == first_before) & (s >= 2))
+            three[rows, :] = join(two, own[rows, :], (last_before == first_own) & (s >= 1))
+        three[foot:, :DK] = near[1, foot:, :DK]
+        three[foot:, DK:] = own[foot:, DK:]
+        for copy in second_copies:
+            copy.start()
+
+    at_tile = pl.ds(pl.multiple_of(i * tile, tile), tile)
     query_tile(
-        doc, i * (x.shape[0] // BLOCK), x, scale, weights, keys, wu, ps_all, causal, out, carried
+        doc, i * (tile // BLOCK), x, scale, weights, keys, wu, ps_all, causal,
+        out.at[:, at_tile, :], carried.at[:, at_tile, :],
     )
 
-
-def query_pass(doc, tokens, gain, scale, wq, keys, wu, ps_all):
+    @pl.when(i == last)
+    def _():
+        for copy in second_copies:
+            copy.wait()
+        first_own, last_before = own[foot : foot + 1, 0:1], far1[foot : foot + 1, DK : DK + 1]
+        first_three, last_four = far1[foot : foot + 1, 0:1], far4[foot : foot + 1, 0:1]
+        for k in range(heads):
+            rows = slice(k * DK, (k + 1) * DK)
+            older = jnp.where(
+                (last_four == first_three) & (s >= 4), dot(far1[rows, :DK], far4[rows, :]), 0.0
+            )
+            state = older + far1[rows, DK:].astype(f32)
+            entering = jnp.where((last_before == first_own) & (s >= 1), state, 0.0).astype(bf16)
+            for g in range(result.shape[0] // STEP):
+                part = slice(g * STEP, (g + 1) * STEP)
+                o = out[k, part, :] + dot(carried[k, part, :], entering)
+                r = lax.rsqrt(jnp.mean(o * o, axis=1, keepdims=True) + norm_eps)
+                result[part, k * DK : (k + 1) * DK] = (o * r * out_gain[...]).astype(bf16)
+
+
+def query_pass(doc, tokens, gain, scale, wq, keys, wu, ps_all, ps, out_gain):
     length, width = tokens.shape
     heads = keys.shape[0]
     steps = length // TILE
     whole = lambda shape: pl.BlockSpec(shape, lambda i, doc: (0,) * len(shape))
     part = lambda *tail: pl.BlockSpec((heads, TILE) + tail, lambda i, doc: (0, i) + (0,) * len(tail))
+    message = (heads * DK + 16, 2 * DK)
     return pl.pallas_call(
         query_kernel,
         grid_spec=pltpu.PrefetchScalarGridSpec(
@@ -332,75 +409,173 @@
                 whole(wq.shape),
                 part(DK),
                 part(2 * DK),
-                pl.BlockSpec(
-                    (heads, TILE // DK, DK, 2 * DK), lambda i, doc: (0, i, 0, 0)
-                ),
+                pl.BlockSpec((heads, TILE // DK, DK, 2 * DK), lambda i, doc: (0, i, 0, 0)),
+                whole(ps.shape),
+                whole(out_gain.shape),
             ],
-            out_specs=[part(DK), part(DK)],
-            scratch_shapes=[pltpu.VMEM(wq.shape, bf16), pltpu.VMEM((STEP, STEP), f32)],
+            out_specs=whole((length, heads * DK)),
+            scratch_shapes=[
+                pltpu.VMEM(wq.shape, bf16),
+                pltpu.VMEM((STEP, STEP), f32),
+                pltpu.VMEM((heads, length, DK), f32),
+                pltpu.VMEM((heads, length, DK), bf16),
+                pltpu.VMEM(message, bf16),
+                pltpu.VMEM((2,) + message, bf16),
+                pltpu.VMEM(message, bf16),
+                pltpu.VMEM(message, bf16),
+                pltpu.VMEM((message[0], DK), bf16),
+                pltpu.SemaphoreType.DMA((4,)),
+                pltpu.SemaphoreType.DMA((4,)),
+            ],
         ),
-        out_shape=[
-            jax.ShapeDtypeStruct((heads, length, DK), f32),
-            jax.ShapeDtypeStruct((heads, length, DK), bf16),
-        ],
-        compiler_params=pltpu.CompilerParams(vmem_limit_bytes=56 << 20),
+        out_shape=jax.ShapeDtypeStruct((length, heads * DK), bf16),
+        compiler_params=pltpu.CompilerParams(
+            vmem_limit_bytes=56 << 20, collective_id=0, has_side_effects=True
+        ),
         cost_estimate=pl.CostEstimate(
             flops=2 * length * width * 3 * DK, bytes_accessed=14 << 20, transcendentals=0
         ),
         name="query_pass",
-    )(doc, tokens, gain, scale, wq, keys, wu, ps_all)
-
-
-def output_kernel(out, carried, incoming, gain, weight, partial):
-    columns = []
-    for h in range(out.shape[0]):
-        o = out[h] + dot(carried[h], incoming[h])
-        scale = lax.rsqrt(jnp.mean(o * o, axis=1, keepdims=True) + norm_eps)
-        columns.append((o * scale * gain[...]).astype(bf16))
-    partial[...] = dot(jnp.concatenate(columns, axis=1), weight[...]).astype(bf16)
-
-
-def output_pass(out, carried, incoming, gain, weight):
-    heads, length, _ = out.shape
+    )(doc, tokens, gain, scale, wq, keys, wu, ps_all, ps, out_gain)
+
+
+SUBS = 2
+
+
+def mix_kernel(
+    normed, full, out, gath, w, obuf,
+    w_sem, there_s, there_r, share_s, share_r, back_s, back_r,
+):
+    s, h = lax.axis_index("seq"), lax.axis_index("head")
+    chips = lax.axis_size("head") // 2
+    y, c = h // 2, lax.rem(h, 2)
+    length, width = normed.shape
+    part = length // chips
+    sub = part // SUBS
+    chip = lambda d: lax.rem(y + d + chips, chips)
+    away = lambda d: peer(s, chip(d) * 2 + c)
+    beside = peer(s, y * 2 + 1 - c)
+
+    def columns(chip_at, core):
+        return pl.ds(pl.multiple_of((chip_at * 2 + core) * width, width), width)
+
+    def rows(chip_at, r):
+        return pl.ds(pl.multiple_of(chip_at * part + r * sub, sub), sub)
+
+    barrier = pltpu.get_barrier_semaphore()
+    for d in range(1, chips):
+        pl.semaphore_signal(barrier, inc=1, **away(d))
+    pl.semaphore_signal(barrier, inc=1, **beside)
+    loads = []
+    for d in range(chips):
+        loads.append(
+            pltpu.make_async_copy(
+                full.at[:, columns(chip(d), c)], w.at[:, d * width : (d + 1) * width], w_sem.at[d]
+            )
+        )
+    for load in loads:
+        load.start()
+    pl.semaphore_wait(barrier, chips)
+
+    def there(r, d):
+        return pltpu.make_async_remote_copy(
+            src_ref=normed.at[rows(chip(d), r), :],
+            dst_ref=gath.at[r * sub : (r + 1) * sub, columns(y, c)],
+            send_sem=there_s.at[r, d],
+            recv_sem=there_r.at[r, d],
+            **away(d),
+        )
+
+    def share(r, d):
+        at = (slice(r * sub, (r + 1) * sub), columns(chip(-d), c))
+        src = normed.at[rows(y, r), :] if d == 0 else gath.at[at]
+        return pltpu.make_async_remote_copy(
+            src_ref=src,
+            dst_ref=gath.at[at],
+            send_sem=share_s.at[r, d],
+            recv_sem=share_r.at[r, d],
+            **beside,
+        )
+
+    def back(r, d):
+        return pltpu.make_async_remote_copy(
+            src_ref=obuf.at[r, d],
+            dst_ref=out.at[rows(y, r), :],
+            send_sem=back_s.at[r, d],
+            recv_sem=back_r.at[r, d],
+            **away(d),
+        )
+
+    order = [2, 1, 3]
+    for r in range(SUBS):
+        for d in order:
+            there(r, d).start()
+    for r in range(SUBS):
+        share(r, 0).start()
+        gath[r * sub : (r + 1) * sub, columns(y, c)] = normed[rows(y, r), :]
+    for r in range(SUBS):
+        for d in [1, 3, 2]:
+            there(r, d).wait_recv()
+            share(r, d).start()
+        for d in range(chips):
+            share(r, d).wait_recv()
+        if r == 0:
+            for load in loads:
+                load.wait()
+        block = gath[r * sub : (r + 1) * sub, :]
+        for d in order:
+            obuf[r, d] = dot(block, w[:, d * width : (d + 1) * width]).astype(bf16)
+            back(r, d).start()
+        out[rows(y, r), :] = dot(block, w[:, :width]).astype(bf16)
+    for r in range(SUBS):
+        for d in order:
+            there(r, d).wait_send()
+        for d in range(chips):
+            share(r, d).wait_send()
+    for r in range(SUBS):
+        for d in order:
+            back(r, d).wait()
+
+
+def mix_pass(normed, full):
+    length, width = normed.shape
+    chips = full.shape[0] // width // 2
+    part = length // chips
+    sub = part // SUBS
+    dma = lambda *shape: pltpu.SemaphoreType.DMA(shape)
+    vmem = pl.BlockSpec(memory_space=pltpu.VMEM)
     return pl.pallas_call(
-        output_kernel,
-        grid=(length // STEP,),
-        in_specs=[
-            pl.BlockSpec((heads, STEP, DK), lambda i: (0, i, 0)),
-            pl.BlockSpec((heads, STEP, DK), lambda i: (0, i, 0)),
-            pl.BlockSpec(incoming.shape, lambda i: (0, 0, 0)),
-            pl.BlockSpec((1, DK), lambda i: (0, 0)),
-            pl.BlockSpec(weight.shape, lambda i: (0, 0)),
+        mix_kernel,
+        in_specs=[vmem, pl.BlockSpec(memory_space=pl.ANY)],
+        out_specs=vmem,
+        out_shape=jax.ShapeDtypeStruct((length, width), bf16),
+        scratch_shapes=[
+            pltpu.VMEM((part, full.shape[0]), bf16),
+            pltpu.VMEM((full.shape[0], chips * width), bf16),
+            pltpu.VMEM((SUBS, chips, sub, width), bf16),
+            dma(chips),
+            dma(SUBS, chips),
+            dma(SUBS, chips),
+            dma(SUBS, chips),
+            dma(SUBS, chips),
+            dma(SUBS, chips),
+            dma(SUBS, chips),
         ],
-        out_specs=pl.BlockSpec((STEP, weight.shape[1]), lambda i: (i, 0)),
-        out_shape=jax.ShapeDtypeStruct((length, weight.shape[1]), bf16),
-        compiler_params=pltpu.CompilerParams(vmem_limit_bytes=32 << 20),
-        name="output_pass",
-    )(out, carried, incoming, gain, weight)
-
-
-def passed_along(block, axis):
-    route = [(i, i + 1) for i in range(lax.axis_size(axis) - 1)]
-    return lax.ppermute(block, axis, route)
+        compiler_params=pltpu.CompilerParams(
+            vmem_limit_bytes=56 << 20, collective_id=1, has_side_effects=True
+        ),
+        name="mix_pass",
+    )(normed, full)
 
 
 def local(tokens, norm_gain, wq, wk, wv, wb, out_gain, wo, block_doc):
-    count = block_doc.shape[0]
     gain = norm_gain[None, :]
+    full = lax.all_gather(wo, "head", axis=0, tiled=True)
     keys, wu, ps_all, ps, scale = keys_pass(block_doc, tokens, gain, wk, wv, wb)
-    out, carried = query_pass(block_doc, tokens, gain, scale, wq, keys, wu, ps_all)
-    transit, state = ps[:, :, :DK].astype(f32), ps[:, :, DK:].astype(f32)
-    first = block_doc[0:1].astype(f32)
-    last = block_doc[count - 1 : count].astype(bf16)
-    before = passed_along(last, "seq").astype(f32)
-    follows = (before[0] == first[0]) & (lax.axis_index("seq") > 0)
-    incoming = jnp.zeros_like(state)
-    for turn in range(MOST_BLOCKS // count):
-        end = state if turn == 0 else jnp.einsum("hde,hef->hdf", transit, incoming) + state
-        got = passed_along(end.astype(bf16), "seq").astype(f32)
-        incoming = jnp.where(follows, got, 0.0)
-    partial = output_pass(out, carried, incoming.astype(bf16), out_gain[None, :], wo)
-    return lax.psum_scatter(partial, "head", scatter_dimension=1, tiled=True)
+    normed = query_pass(
+        block_doc, tokens, gain, scale, wq, keys, wu, ps_all, ps, out_gain[None, :]
+    )
+    return mix_pass(normed, full)
 
 
 def solution(mesh):

time: 177 us -> 104 us (0.59)
  waiting for transfers between devices: 73.1 us -> 0.73 us
  Pallas kernels: 46.2 us -> 85.2 us
  starting transfers between devices: 28.6 us -> 0.01 us
  local copies, waits for them, and re-layouts: 9.3 us -> 4.04 us
  matrix products: 5.11 us -> 0 us
    reduce_scatter x1 -> x0, waiting for transfers between devices: 67.5 us -> none  [local(): return lax.psum_scatter(partial, 'head', scatter_dimension=1, tiled=True)]
    ppermute x7 -> x0, starting transfers between devices: 28.6 us -> none  [passed_along(): return lax.ppermute(block, axis, route)]
    pallas_call x1, Pallas kernels: 5.49 us -> 31.4 us  [mix_pass(): pl.pallas_call(mix_kernel, in_specs=[vmem, pl.BlockSpec(memory_space=pl.A...]
    pallas_call x1, Pallas kernels: 11.1 us -> 24.2 us  [query_pass(): pl.pallas_call(query_kernel, grid_spec=pltpu.PrefetchScalarGridSpec(num_s...]
    ppermute x7 -> x0, waiting for transfers between devices: 5.61 us -> none  [passed_along(): return lax.ppermute(block, axis, route)]
    dot_general x5 -> x0, matrix products: 5.11 us -> none  [local(): jnp.einsum('hde,hef->hdf', transit, incoming) + state]
    unnamed x13 -> x2, local copies, waits for them, and re-layouts: 7.79 us -> 4.04 us
  transfers between devices with their start and end apart: 8 -> 1, of which waited for: 6 -> 0; matrix products, arithmetic and copies ran while one was open for 0% -> 2% of each run, Pallas kernels for 6% -> 52%
where the time goes in v3:
time: 104 us; the launch traced here: 103 us
  Pallas kernels  85.2 us (82%)
  between operations  13.4 us (13%)
  local copies, waits for them, and re-layouts  4.04 us (4%)
    pallas_call x1, Pallas kernels, mix_pass(): pl.pallas_call(mix_kernel, in_specs=[vmem, pl.BlockSpec(memory_space=pl.A...  31.4 us
    pallas_call x1, Pallas kernels, keys_pass(): pl.pallas_call(keys_kernel, grid_spec=pltpu.PrefetchScalarGridSpec(num_sc...  29.6 us
    pallas_call x1, Pallas kernels, query_pass(): pl.pallas_call(query_kernel, grid_spec=pltpu.PrefetchScalarGridSpec(num_s...  24.2 us
    unnamed x2, local copies, waits for them, and re-layouts  4.04 us
  transfers between devices with their start and end apart: 1, of which 0 were waited for; matrix products, arithmetic and copies ran while one was open for 2% of the time, Pallas kernels for 52%

profile of v3, /device:TPU:1, one launch (start us, length us, event | category | flops | bytes accessed | tf_op | source)
XLA Modules:
  0.0 103.4 jit_solution(8195593402355288638)
XLA Ops:
  6.5 0.0 all-gather.2.cloned.1.call-start
  6.5 0.7 all-gather.2.cloned.1.call-update
  7.3 1.8 %copy.10.wb = bf16[2048,2]{1,0:T(8,128)(2,1)} copy(bf16[2048,2]{0,1:T(2,128)(2,1)} %param.14) | data formatting | bytes 16384 | tf_op args[5]
  9.0 29.6 %keys_pass.1 = (bf16[2,2048,128]{2,1,0:T(8,128)(2,1)}, bf16[2,2048,256]{2,1,0:T(8,128)(2,1)}, bf16[2,16,128,256]{3,2,1,0:T(8,128)(2,1)}, bf16[2,128,256]{2,1,0:T(8,128)(2,1)}, f32[2048,128]{1,0:T(8,128)}) custom-call(s32[32]{0:T(128)} %doc.3, bf16[2048,2048]{1,0:T(8,128)(2,1)} %x.3, f32[1,2048]{1,0:T(1,128)} %bitcast.2, bf16[2048,256]{1,0:T(8,128)(2,1)} %wk.1, ...), custom_call_target="tpu_custom_call" | custom-call | flops 5368709120 | bytes 20971520 | tf_op jit(solution)/shard_map/keys_pass/pallas_call | solution.py:229
  38.6 24.2 %query_pass.1.normed = bf16[2048,256]{1,0:T(8,128)(2,1)} custom-call(s32[32]{0:T(128)} %doc.3, bf16[2048,2048]{1,0:T(8,128)(2,1)} %x.3, f32[1,2048]{1,0:T(1,128)} %bitcast.3, f32[2048,128]{1,0:T(8,128)} %get-tuple-element.10.scale, bf16[2048,256]{1,0:T(8,128)(2,1)} %wq.1, bf16[2,2048,128]{2,1,0:T(8,128)(2,1)} %get-tuple-element.11.keys, ...), custom_call_target="tpu_custom_call" | custom-call | flops 3221225472 | bytes 14680064 | tf_op jit(solution)/shard_map/query_pass/pallas_call | solution.py:400
  62.8 0.0 all-gather.2.cloned.1.call-done.full
  62.9 31.4 %mix_pass.1 = bf16[2048,256]{1,0:T(8,128)(2,1)} custom-call(bf16[2048,256]{1,0:T(8,128)(2,1)} %query_pass.1.normed, bf16[2048,2048]{1,0:T(8,128)(2,1)} %all-gather.2.cloned.1.call-done.full), custom_call_target="tpu_custom_call" | custom-call | tf_op jit(solution)/shard_map/mix_pass/pallas_call | solution.py:547
  94.2 2.3 %copy.12 = bf16[2048,256]{1,0:T(8,128)(2,1)} copy(bf16[2048,256]{1,0:T(8,128)(2,1)} %mix_pass.1) | data formatting | bytes 2097152
Async XLA Ops:
  6.5 56.3 %all-gather.2.cloned.1.call-start = ((), (), s32[]{:S(2)}) async-start(), calls=%async_computation | async-start | bytes 9437184 | tf_op jit(solution)/shard_map/all_gather | solution.py:573
Sparse Core Ops, SparseCore 0:
  9.1 53.3 all-gather.1

commit v4 on v2

v4 whole, which is shorter than its diff:
```python
import jax
import jax.numpy as jnp
from jax import lax
from jax.experimental import pallas as pl
from jax.experimental.pallas import tpu as pltpu
from jax.sharding import PartitionSpec as P

norm_eps = 1e-05
key_eps = 1e-06
BLOCK = 64
DK = 128
STEP = 256
TILE = 512
SIDE = 4
SPREAD_AT = 2
SUBS = 2
f32 = jnp.float32
bf16 = jnp.bfloat16
LEVELS = (2, 4, 8, 16, 32, 64)


def dot(a, b):
    return jnp.dot(a, b, preferred_element_type=f32)


def dot_nt(a, b):
    return lax.dot_general(a, b, (((1,), (1,)), ((), ())), preferred_element_type=f32)


def dot_tn(a, b):
    return lax.dot_general(a, b, (((0,), (0,)), ((), ())), preferred_element_type=f32)


def unit(values):
    act = values * jax.nn.sigmoid(values)
    return act * lax.rsqrt(jnp.sum(act * act, axis=1, keepdims=True) + key_eps)


def peer(s, h):
    return dict(device_id=(s, h), device_id_type=pl.DeviceIdType.MESH)


def fill_masks(strict, causal, pair, off):
    shape = (STEP, STEP)
    row = lax.broadcasted_iota(jnp.int32, shape, 0)
    col = lax.broadcasted_iota(jnp.int32, shape, 1)
    same = (row // DK) == (col // DK)
    strict[...] = jnp.where(same & (row > col), 1.0, 0.0).astype(f32)
    causal[...] = jnp.where(same & (row >= col), 1.0, 0.0).astype(f32)
    pair[0] = jnp.where((row // 2 == col // 2) & (row > col), 1.0, 0.0).astype(bf16)
    pair[1] = jnp.where(row == col, 1.0, 0.0).astype(bf16)
    for n, s in enumerate(LEVELS):
        hit = (row // (2 * s) == col // (2 * s)) & (row // s > col // s)
        off[n] = jnp.where(hit, 1.0, 0.0).astype(bf16)


def scaled_weight(weight, gain):
    column = jnp.transpose(jnp.broadcast_to(gain[...], (DK, gain.shape[1])))
    parts = [
        weight[:, n * DK : (n + 1) * DK].astype(f32) * column for n in range(weight.shape[1] // DK)
    ]
    return jnp.concatenate(parts, axis=1).astype(bf16)


def doc_masks(doc, at):
    d = [doc[at + j] for j in range(4)]
    before = doc[jnp.maximum(at - 1, 0)]
    link = [
        jnp.where((before == d[0]) | (at == 0), 1.0, 0.0).astype(f32),
        jnp.where(d[1] == d[2], 1.0, 0.0).astype(f32),
    ]
    join = [
        jnp.where(d[0] == d[1], 1.0, 0.0).astype(f32),
        jnp.where(d[2] == d[3], 1.0, 0.0).astype(f32),
    ]
    row = lax.broadcasted_iota(jnp.int32, (STEP, 1), 0)
    second = (row % DK) >= BLOCK
    join_r = jnp.where(row >= DK, join[1], join[0])
    link_r = jnp.where(row >= DK, link[1], link[0])
    enters = jnp.where(second, link_r * join_r, link_r)
    leaves = jnp.where(second, 1.0, join_r)
    cross = jnp.where(second, join_r, 1.0)
    col = lax.broadcasted_iota(jnp.int32, (1, STEP), 1)
    full = jnp.where((col % DK) < BLOCK, cross, 1.0)
    return enters, leaves, full, [link[c] * join[c] for c in range(2)]


def interleave(main, side, every):
    count = 0
    for _ in main:
        count += 1
        if count % every == 0:
            next(side, None)
    for _ in side:
        pass


def project_keys(x, scale_out, weights, keys_at, vbuf, bbuf, slot):
    halves = x.shape[0] // STEP
    scales = []
    for m in range(halves):
        rows = slice(m * STEP, (m + 1) * STEP)
        floats = x[rows, :].astype(f32)
        r = lax.rsqrt(jnp.mean(floats * floats, axis=1, keepdims=True) + norm_eps)
        scales.append(r)
        scale_out[rows, :] = jnp.broadcast_to(r, (STEP, DK))
        yield
        b = dot(x[rows, :], weights[:, 4 * DK :]) * r
        bbuf[slot, rows, :] = jax.nn.sigmoid(b)
        yield
        for h in range(2):
            kv = dot(x[rows, :], weights[:, 2 * h * DK : 2 * (h + 1) * DK]) * r
            keys_at[h, rows, :] = unit(kv[:, :DK]).astype(bf16)
            vbuf[slot, h, rows, :] = kv[:, DK:]
            yield


def solve_keys(doc, at, keys_at, vbuf, bbuf, slot, ps, masks, wu_out, ps_all):
    strict, pair, off = masks
    halves = keys_at.shape[1] // STEP
    groups = [(h, g) for g in range(halves) for h in range(2)]
    dm = [doc_masks(doc, at + 4 * g) for g in range(halves)]
    keys, a_hi, a_lo, xb, t, right, y, wu = {}, {}, {}, {}, {}, {}, {}, {}
    beta = {}
    for h, g in groups:
        rows = slice(g * STEP, (g + 1) * STEP)
        keys[h, g] = keys_at[h, rows, :]
        beta[h, g] = bbuf[slot, rows, h : h + 1]
        a = dot_nt(keys[h, g], keys[h, g]) * beta[h, g] * (strict[...] * dm[g][2])
        hi = a.astype(bf16)
        a_hi[h, g] = hi
        a_lo[h, g] = (a - hi.astype(f32)).astype(bf16)
        xb[h, g] = pair[1] - hi * pair[0]
        yield
    for n in range(len(LEVELS)):
        for at_group in groups:
            t[at_group] = dot(a_hi[at_group] * off[n], xb[at_group]).astype(bf16)
        yield
        for at_group in groups:
            xb[at_group] = xb[at_group] - dot(xb[at_group], t[at_group]).astype(bf16)
        yield
    for h, g in groups:
        rows = slice(g * STEP, (g + 1) * STEP)
        b = beta[h, g]
        right[h, g] = jnp.concatenate(
            [(b * dm[g][0]) * keys[h, g].astype(f32), b * vbuf[slot, h, rows, :]], axis=1
        )
        y[h, g] = dot(xb[h, g], right[h, g].astype(bf16)).astype(bf16)
    yield
    left = {}
    for k in groups:
        rest = right[k] - y[k].astype(f32) - dot(a_hi[k], y[k]) - dot(a_lo[k], y[k])
        left[k] = rest.astype(bf16)
    yield
    for h, g in groups:
        wu[h, g] = (y[h, g].astype(f32) + dot(xb[h, g], left[h, g])).astype(bf16)
        wu_out[h, g * STEP : (g + 1) * STEP, :] = wu[h, g]
    yield
    step = {}
    for h, g in groups:
        k_end = (keys[h, g].astype(f32) * dm[g][1]).astype(bf16)
        for c in range(2):
            rows = slice(c * DK, (c + 1) * DK)
            step[h, g, c] = dot_tn(k_end[rows], wu[h, g][rows])
    yield
    for g in range(halves):
        for c in range(2):
            for h in range(2):
                state = ps[h]
                sb = state.astype(bf16)
                ps_all[h, 2 * g + c] = sb
                move = step[h, g, c]
                moved = dot(move[:, :DK].astype(bf16), sb)
                gain = jnp.concatenate([jnp.zeros((DK, DK), f32), move[:, DK:]], axis=1)
                ps[h] = dm[g][3][c] * state - moved + gain
            yield


def query_tile(doc, at, x, scale, weights, keys, wu, ps_all, causal, out, carried):
    groups = [(h, g) for g in range(x.shape[0] // STEP) for h in range(2)]
    dm = [doc_masks(doc, at + 4 * g) for g in range(x.shape[0] // STEP)]
    qb, mixed, scores = {}, {}, {}
    for g in range(x.shape[0] // STEP):
        rows = slice(g * STEP, (g + 1) * STEP)
        both = dot(x[rows, :], weights[...]) * scale[rows, 0:1]
        for h in range(2):
            qb[h, g] = unit(both[:, h * DK : (h + 1) * DK]).astype(bf16)
    for h, g in groups:
        rows = slice(g * STEP, (g + 1) * STEP)
        s = dot_nt(qb[h, g], keys[h, rows, :]) * (causal[...] * dm[g][2])
        scores[h, g] = s.astype(bf16)
    for h, g in groups:
        rows = slice(g * STEP, (g + 1) * STEP)
        mixed[h, g] = dot(scores[h, g], wu[h, rows, :])
    for h, g in groups:
        reach = (dm[g][0] * qb[h, g].astype(f32) - mixed[h, g][:, :DK]).astype(bf16)
        for c in range(2):
            rows = slice(c * DK, (c + 1) * DK)
            to = slice(g * STEP + c * DK, g * STEP + (c + 1) * DK)
            seen = dot(reach[rows], ps_all[h, 2 * g + c])
            carried[h, to, :] = seen[:, :DK].astype(bf16)
            out[h, to, :] = mixed[h, g][rows, DK:] + seen[:, DK:]


class Place:
    def __init__(self):
        self.s, h = lax.axis_index("seq"), lax.axis_index("head")
        self.length = lax.axis_size("seq")
        self.chips = lax.axis_size("head") // 2
        self.y, self.c = h // 2, lax.rem(h, 2)
        self.outer, self.inner = self.s // SIDE, lax.rem(self.s, SIDE)

    def later(self, d):
        return peer(lax.rem(self.s + d + self.length, self.length), self.y * 2 + self.c)

    def chip(self, d, core):
        return peer(self.s, lax.rem(self.y + d + self.chips, self.chips) * 2 + core)

    def beside(self):
        return self.chip(0, 1 - self.c)

    def along(self, axis, d):
        if axis == 0:
            s = lax.rem(self.outer + d + SIDE, SIDE) * SIDE + self.inner
        else:
            s = self.outer * SIDE + lax.rem(self.inner + d + SIDE, SIDE)
        return peer(s, self.y * 2 + self.c)

    def peers(self):
        found = [self.chip(d, core) for d in range(1, self.chips) for core in range(2)]
        found.append(self.beside())
        found += [self.along(a, d) for a in range(2) for d in range(1, SIDE)]
        return found + [self.later(d) for d in (1, -1, 2, -2, 4, -4)]


class WeightGather:
    def __init__(self, me, wo, w, over_s, over_r, near_s, ring_s, ring_r):
        self.me, self.wo, self.w = me, wo, w
        self.over_s, self.over_r, self.near_s = over_s, over_r, near_s
        self.ring_s, self.ring_r = ring_s, ring_r
        self.depth, self.half = w.shape[1], w.shape[2]
        self.quarter, self.wide = self.depth // SIDE, self.half // 2

    def rows(self, axis):
        q = self.me.outer if axis == 0 else self.me.inner
        return pl.ds(pl.multiple_of(q * self.quarter, self.quarter), self.quarter)

    def over(self, d, core, axis, origin):
        start = core * self.half + axis * self.wide
        block = (self.me.chips - d) * 2 + origin
        return pltpu.make_async_remote_copy(
            src_ref=self.wo.at[self.rows(axis), start : start + self.wide],
            dst_ref=self.w.at[block, self.rows(axis), axis * self.wide : (axis + 1) * self.wide],
            send_sem=self.over_s.at[d - 1, core, axis],
            recv_sem=self.over_r.at[d - 1, origin, axis],
            **self.me.chip(d, core),
        )

    def columns(self, core):
        return pl.ds(pl.multiple_of(core * self.half, self.half), self.half)

    def pair(self):
        return pltpu.make_async_remote_copy(
            src_ref=self.wo.at[:, self.columns(1 - self.me.c)],
            dst_ref=self.w.at[self.me.c],
            send_sem=self.near_s.at[0],
            recv_sem=self.near_s.at[1],
            **self.me.beside(),
        )

    def own(self):
        return pltpu.make_async_copy(
            self.wo.at[:, self.columns(self.me.c)], self.w.at[self.me.c], self.near_s.at[2]
        )

    def ring(self, axis, d):
        at = self.w.at[2:, self.rows(axis), axis * self.wide : (axis + 1) * self.wide]
        return pltpu.make_async_remote_copy(
            src_ref=at,
            dst_ref=at,
            send_sem=self.ring_s.at[axis, d - 1],
            recv_sem=self.ring_r.at[axis, d - 1],
            **self.me.along(axis, d),
        )

    def each_over(self):
        return [(d, k, a) for d in (2, 1, 3) for k in range(2) for a in range(2)]

    def each_ring(self):
        return [(a, d) for d in (2, 1, 3) for a in range(2)]

    def begin(self):
        for d, core, axis in self.each_over():
            self.over(d, core, axis, self.me.c).start()
        self.pair().start()
        self.own().start()

    def spread(self):
        for d, core, axis in self.each_over():
            self.over(d, core, axis, core).wait_recv()
        for at in self.each_ring():
            self.ring(*at).start()

    def finish(self):
        for d, core, axis in self.each_over():
            self.over(d, core, axis, self.me.c).wait_send()
        self.pair().wait()
        self.own().wait()
        for at in self.each_ring():
            self.ring(*at).wait()


def join(first, then, follows):
    moved = jnp.where(follows, dot(then[:, :DK], first), 0.0)
    gain = jnp.concatenate([jnp.zeros((DK, DK), f32), then[:, DK:].astype(f32)], axis=1)
    return (moved + gain).astype(bf16)


class StateExchange:
    def __init__(self, me, own, near, three, far1, far4, send, recv):
        self.me = me
        self.own, self.near, self.three, self.far1, self.far4 = own, near, three, far1, far4
        self.send, self.recv = send, recv
        self.foot = own.shape[0] - 16

    def move(self, src, dst, at, d):
        return pltpu.make_async_remote_copy(
            src_ref=src, dst_ref=dst, send_sem=self.send.at[at], recv_sem=self.recv.at[at],
            **self.me.later(d),
        )

    def first_round(self):
        return [self.move(self.own, self.near.at[0], 0, 1), self.move(self.own, self.near.at[1], 1, 2)]

    def second_round(self):
        return [
            self.move(self.three, self.far1, 2, 1),
            self.move(self.three.at[:, DK:], self.far4, 3, 4),
        ]

    def begin(self, ps, first_doc, last_doc):
        foot = self.foot
        for k in range(ps.shape[0]):
            self.own[k * DK : (k + 1) * DK, :] = ps[k].astype(bf16)
        self.own[foot:, :DK] = jnp.full((16, DK), first_doc.astype(f32)).astype(bf16)
        self.own[foot:, DK:] = jnp.full((16, DK), last_doc.astype(f32)).astype(bf16)
        for copy in self.first_round():
            copy.start()

    def again(self):
        for copy in self.first_round():
            copy.wait()
        foot, own, near, s = self.foot, self.own, self.near, self.me.s
        first_own, last_one = own[foot : foot + 1, 0:1], near[0, foot : foot + 1, DK : DK + 1]
        first_one, last_two = near[0, foot : foot + 1, 0:1], near[1, foot : foot + 1, DK : DK + 1]
        for k in range(foot // DK):
            rows = slice(k * DK, (k + 1) * DK)
            two = join(near[1, rows, :], near[0, rows, :], (last_two == first_one) & (s >= 2))
            self.three[rows, :] = join(two, own[rows, :], (last_one == first_own) & (s >= 1))
        self.three[foot:, :DK] = near[1, foot:, :DK]
        self.three[foot:, DK:] = own[foot:, DK:]
        for copy in self.second_round():
            copy.start()

    def entering(self):
        for copy in self.second_round():
            copy.wait()
        foot, far1, far4, s = self.foot, self.far1, self.far4, self.me.s
        first_own, last_one = self.own[foot : foot + 1, 0:1], far1[foot : foot + 1, DK : DK + 1]
        first_three, last_four = far1[foot : foot + 1, 0:1], far4[foot : foot + 1, 0:1]
        states = []
        for k in range(foot // DK):
            rows = slice(k * DK, (k + 1) * DK)
            older = jnp.where(
                (last_four == first_three) & (s >= 4), dot(far1[rows, :DK], far4[rows, :]), 0.0
            )
            state = older + far1[rows, DK:].astype(f32)
            states.append(jnp.where((last_one == first_own) & (s >= 1), state, 0.0).astype(bf16))
        return states


class Mixer:
    def __init__(self, me, normed, gath, w, obuf, result, there_s, there_r, share_s, share_r, back_s, back_r):
        self.me, self.normed, self.gath, self.w = me, normed, gath, w
        self.obuf, self.result = obuf, result
        self.there_s, self.there_r, self.share_s, self.share_r = there_s, there_r, share_s, share_r
        self.back_s, self.back_r = back_s, back_r
        self.width = normed.shape[1]
        self.part = normed.shape[0] // me.chips
        self.sub = self.part // SUBS

    def rows(self, d, r):
        chip_at = lax.rem(self.me.y + d + self.me.chips, self.me.chips)
        return pl.ds(pl.multiple_of(chip_at * self.part + r * self.sub, self.sub), self.sub)

    def spot(self, r, d, core):
        block = (self.me.chips - d) % self.me.chips * 2 + core
        lanes = pl.ds(pl.multiple_of(block * self.width, self.width), self.width)
        return self.gath.at[r * self.sub : (r + 1) * self.sub, lanes]

    def there(self, r, d):
        return pltpu.make_async_remote_copy(
            src_ref=self.normed.at[self.rows(d, r), :],
            dst_ref=self.spot(r, d, self.me.c),
            send_sem=self.there_s.at[r, d],
            recv_sem=self.there_r.at[r, d],
            **self.me.chip(d, self.me.c),
        )

    def share(self, r, d):
        at = self.spot(r, d, self.me.c)
        return pltpu.make_async_remote_copy(
            src_ref=self.normed.at[self.rows(0, r), :] if d == 0 else at,
            dst_ref=at,
            send_sem=self.share_s.at[r, d],
            recv_sem=self.share_r.at[r, d],
            **self.me.beside(),
        )

    def back(self, r, t, e):
        return pltpu.make_async_remote_copy(
            src_ref=self.obuf.at[r, t],
            dst_ref=self.result.at[self.rows(0, r), :],
            send_sem=self.back_s.at[r, t],
            recv_sem=self.back_r.at[r, e],
            **peer(self.me.s, 2 * self.me.chips // 2 * self.me.c + t),
        )

    def home(self, r, t):
        return pltpu.make_async_copy(
            self.obuf.at[r, t], self.result.at[self.rows(0, r), :], self.back_s.at[r, t]
        )

    def target(self, t):
        at = self.me.chips * self.me.c + t
        far = lax.rem(at // 2 - self.me.y + self.me.chips, self.me.chips)
        return far, at == self.me.y * 2 + self.me.c

    def run(self):
        me, chips = self.me, self.me.chips
        order = [2, 1, 3]
        for r in range(SUBS):
            self.share(r, 0).start()
            self.spot(r, 0, me.c)[...] = self.normed[self.rows(0, r), :]
        for r in range(SUBS):
            for d in [1, 3, 2]:
                self.there(r, d).wait_recv()
                self.share(r, d).start()
            for d in range(chips):
                self.share(r, d).wait_recv()
            block = self.gath[r * self.sub : (r + 1) * self.sub, :]
            w = self.w[...].reshape(self.w.shape[0] * self.w.shape[1], self.w.shape[2])
            for t in range(chips):
                cut = w[:, t * self.width : (t + 1) * self.width]
                self.obuf[r, t] = dot(block, cut).astype(bf16)
                far, mine = self.target(t)

                @pl.when(jnp.logical_not(mine))
                def _():
                    self.back(r, t, far).start()

                @pl.when(mine)
                def _():
                    self.home(r, t).start()

        for r in range(SUBS):
            for d in order:
                self.there(r, d).wait_send()
            for d in range(chips):
                self.share(r, d).wait_send()
            for t in range(chips):
                far, mine = self.target(t)

                @pl.when(jnp.logical_not(mine))
                def _():
                    self.back(r, t, far).wait_send()

                @pl.when(mine)
                def _():
                    self.home(r, t).wait()

            for e in range(1, chips):
                self.back(r, 0, e).wait_recv()

            @pl.when(me.c != me.y // (chips // 2))
            def _():
                self.back(r, 0, 0).wait_recv()


def layer_kernel(
    doc, x, gain, wk, wv, wb, wq, out_gain, wo, result,
    weights, wqs, keys, vbuf, bbuf, scale, wu, ps_all, ps, strict, causal, pair, off,
    out, carried, own, near, three, far1, far4, normed, gath, w, obuf,
    over_s, over_r, near_s, ring_s, ring_r, st_s, st_r,
    there_s, there_r, share_s, share_r, back_s, back_r,
):
    i = pl.program_id(0)
    tile, count = x.shape[0], doc.shape[0]
    blocks = tile // BLOCK
    tiles = count // blocks
    me = Place()
    gather = WeightGather(me, wo, w, over_s, over_r, near_s, ring_s, ring_r)
    states = StateExchange(me, own, near, three, far1, far4, st_s, st_r)
    mixer = Mixer(
        me, normed, gath, w, obuf, result, there_s, there_r, share_s, share_r, back_s, back_r
    )

    def at_tile(j):
        return pl.ds(pl.multiple_of(j * tile, tile), tile)

    def project():
        at = at_tile(jnp.minimum(i, tiles - 1))
        return project_keys(x, scale.at[at, :], weights, keys.at[:, at, :], vbuf, bbuf, i % 2)

    def solve():
        j = jnp.clip(i - 1, 0, tiles - 1)
        at = at_tile(j)
        chunks = pl.ds(pl.multiple_of(j * (tile // DK), tile // DK), tile // DK)
        return solve_keys(
            doc, j * blocks, keys.at[:, at, :], vbuf, bbuf, (i + 1) % 2, ps,
            (strict, pair, off), wu.at[:, at, :], ps_all.at[:, chunks],
        )

    @pl.when(i == 0)
    def _():
        barrier = pltpu.get_barrier_semaphore()
        for at in me.peers():
            pl.semaphore_signal(barrier, inc=1, **at)
        fill_masks(strict, causal, pair, off)
        sk, sv = scaled_weight(wk, gain), scaled_weight(wv, gain)
        for h in range(2):
            weights[:, 2 * h * DK : (2 * h + 1) * DK] = sk[:, h * DK : (h + 1) * DK]
            weights[:, (2 * h + 1) * DK : (2 * h + 2) * DK] = sv[:, h * DK : (h + 1) * DK]
        rest = jnp.zeros((DK - wb.shape[0], wb.shape[1]), f32)
        padded = jnp.concatenate([wb[...].astype(f32) * gain[...], rest], axis=0)
        weights[:, 4 * DK :] = jnp.transpose(padded).astype(bf16)
        pl.semaphore_wait(barrier, len(me.peers()))
        gather.begin()
        row = lax.broadcasted_iota(jnp.int32, (DK, 2 * DK), 0)
        col = lax.broadcasted_iota(jnp.int32, (DK, 2 * DK), 1)
        for h in range(2):
            ps[h] = jnp.where(row == col, 1.0, 0.0).astype(f32)
        for _ in project():
            pass

    @pl.when(i == SPREAD_AT)
    def _():
        gather.spread()

    @pl.when((i > 0) & (i < tiles))
    def _():
        interleave(solve(), project(), 2)

    @pl.when(i == tiles)
    def _():
        for _ in solve():
            pass
        states.begin(ps, doc[0], doc[count - 1])
        wqs[...] = scaled_weight(wq, gain)

    @pl.when(i == 2 * tiles)
    def _():
        states.again()

    @pl.when(i > tiles)
    def _():
        j = jnp.clip(i - tiles - 1, 0, tiles - 1)
        at = at_tile(j)
        chunks = pl.ds(pl.multiple_of(j * (tile // DK), tile // DK), tile // DK)
        query_tile(
            doc, j * blocks, x, scale.at[at, :], wqs, keys.at[:, at, :], wu.at[:, at, :],
            ps_all.at[:, chunks], causal, out.at[:, at, :], carried.at[:, at, :],
        )

    @pl.when(i == 2 * tiles)
    def _():
        entering = states.entering()
        for r in range(SUBS):
            for d in (2, 1, 3, 0):
                rows = mixer.rows(d, r)
                for k in range(len(entering)):
                    o = out[k, rows, :] + dot(carried[k, rows, :], entering[k])
                    size = lax.rsqrt(jnp.mean(o * o, axis=1, keepdims=True) + norm_eps)
                    normed[rows, k * DK : (k + 1) * DK] = (o * size * out_gain[...]).astype(bf16)
                if d:
                    mixer.there(r, d).start()
        gather.finish()
        mixer.run()


def layer_pass(doc, tokens, gain, wk, wv, wb, wq, out_gain, wo):
    length, width = tokens.shape
    heads = wb.shape[0]
    tiles = length // TILE
    depth = wo.shape[0]
    chips = wo.shape[1] // depth // 2
    part = length // chips
    sub = part // SUBS
    message = (heads * DK + 16, 2 * DK)
    dma = lambda *shape: pltpu.SemaphoreType.DMA(shape)
    whole = lambda shape: pl.BlockSpec(
        shape, lambda i, doc: (0,) * len(shape), pipeline_mode=pl.Buffered(1)
    )
    return pl.pallas_call(
        layer_kernel,
        grid_spec=pltpu.PrefetchScalarGridSpec(
            num_scalar_prefetch=1,
            grid=(2 * tiles + 1,),
            in_specs=[
                pl.BlockSpec(
                    (TILE, width),
                    lambda i, doc: (
                        jnp.where(i > tiles, i - tiles - 1, jnp.minimum(i, tiles - 1)),
                        0,
                    ),
                ),
                whole((1, width)),
                whole(wk.shape),
                whole(wv.shape),
                whole(wb.shape),
                whole(wq.shape),
                whole(out_gain.shape),
                pl.BlockSpec(memory_space=pl.ANY),
            ],
            out_specs=pl.BlockSpec(memory_space=pl.ANY),
            scratch_shapes=[
                pltpu.VMEM((width, 5 * DK), bf16),
                pltpu.VMEM(wq.shape, bf16),
                pltpu.VMEM((heads, length, DK), bf16),
                pltpu.VMEM((2, heads, TILE, DK), f32),
                pltpu.VMEM((2, TILE, DK), f32),
                pltpu.VMEM((length, DK), f32),
                pltpu.VMEM((heads, length, 2 * DK), bf16),
                pltpu.VMEM((heads, length // DK, DK, 2 * DK), bf16),
                pltpu.VMEM((heads, DK, 2 * DK), f32),
                pltpu.VMEM((STEP, STEP), f32),
                pltpu.VMEM((STEP, STEP), f32),
                pltpu.VMEM((2, STEP, STEP), bf16),
                pltpu.VMEM((len(LEVELS), STEP, STEP), bf16),
                pltpu.VMEM((heads, length, DK), f32),
                pltpu.VMEM((heads, length, DK), bf16),
                pltpu.VMEM(message, bf16),
                pltpu.VMEM((2,) + message, bf16),
                pltpu.VMEM(message, bf16),
                pltpu.VMEM(message, bf16),
                pltpu.VMEM((message[0], DK), bf16),
                pltpu.VMEM((length, heads * DK), bf16),
                pltpu.VMEM((part, wo.shape[1]), bf16),
                pltpu.VMEM((2 * chips, depth, wo.shape[1] // 2), bf16),
                pltpu.VMEM((SUBS, chips, sub, depth), bf16),
                dma(chips - 1, 2, 2),
                dma(chips - 1, 2, 2),
                dma(3),
                dma(2, SIDE - 1),
                dma(2, SIDE - 1),
                dma(4),
                dma(4),
            ]
            + [dma(SUBS, chips)] * 6,
        ),
        out_shape=jax.ShapeDtypeStruct((length, heads * DK), bf16),
        compiler_params=pltpu.CompilerParams(
            vmem_limit_bytes=58 << 20, collective_id=0, has_side_effects=True
        ),
        name="layer_pass",
    )(doc, tokens, gain, wk, wv, wb, wq, out_gain, wo)


def local(tokens, norm_gain, wq, wk, wv, wb, out_gain, wo, block_doc):
    return layer_pass(
        block_doc, tokens, norm_gain[None, :], wk, wv, wb.T, wq, out_gain[None, :], wo
    )


def solution(mesh):
    in_specs = (
        P("seq", None),
        P(),
        P(None, "head"),
        P(None, "head"),
        P(None, "head"),
        P(None, "head"),
        P(),
        P("head", None),
        P("seq"),
    )
    return jax.shard_map(
        local, mesh=mesh, in_specs=in_specs, out_specs=P("seq", "head"), check_vma=False
    )
```

time: 177 us -> 82.4 us (0.47)
  waiting for transfers between devices: 73.1 us -> 0 us
  Pallas kernels: 46.2 us -> 79.9 us
  starting transfers between devices: 28.6 us -> 0 us
  between operations: 14.2 us -> 0.01 us
  local copies, waits for them, and re-layouts: 9.3 us -> 2.26 us
  matrix products: 5.11 us -> 0 us
    reduce_scatter x1 -> x0, waiting for transfers between devices: 67.5 us -> none  [local(): return lax.psum_scatter(partial, 'head', scatter_dimension=1, tiled=True)]
    pallas_call x3 -> x1, Pallas kernels: 46.2 us -> 79.9 us  [layer_pass(): pl.pallas_call(layer_kernel, grid_spec=pltpu.PrefetchScalarGridSpec(num_s...]
    ppermute x7 -> x0, starting transfers between devices: 28.6 us -> none  [passed_along(): return lax.ppermute(block, axis, route)]
    ppermute x7 -> x0, waiting for transfers between devices: 5.61 us -> none  [passed_along(): return lax.ppermute(block, axis, route)]
    unnamed x13 -> x1, local copies, waits for them, and re-layouts: 7.79 us -> 2.26 us
    dot_general x5 -> x0, matrix products: 5.11 us -> none  [local(): jnp.einsum('hde,hef->hdf', transit, incoming) + state]
  transfers between devices with their start and end apart: 8 -> 0, of which waited for: 6 -> 0; matrix products, arithmetic and copies ran while one was open for 0% -> 0% of each run, Pallas kernels for 6% -> 0%
where the time goes in v4:
time: 82.4 us; the launch traced here: 82.2 us
  Pallas kernels  79.9 us (97%)
  local copies, waits for them, and re-layouts  2.26 us (3%)
    pallas_call x1, Pallas kernels, layer_pass(): pl.pallas_call(layer_kernel, grid_spec=pltpu.PrefetchScalarGridSpec(num_s...  79.9 us
    unnamed x1, local copies, waits for them, and re-layouts  2.26 us

profile of v4, /device:TPU:1, one launch (start us, length us, event | category | flops | bytes accessed | tf_op | source)
XLA Modules:
  0.0 82.2 jit_solution(6067585343981638003)
XLA Ops:
  0.0 79.9 %layer_pass.1 = bf16[2048,256]{1,0:T(8,128)(2,1)} custom-call(s32[32]{0:T(128)} %doc.1, bf16[2048,2048]{1,0:T(8,128)(2,1)} %x.1, f32[1,2048]{1,0:T(1,128)} %bitcast.3, bf16[2048,256]{1,0:T(8,128)(2,1)} %wk.1, bf16[2048,256]{1,0:T(8,128)(2,1)} %wv.1, bf16[2,2048]{1,0:T(2,128)(2,1)} %bitcast.4, bf16[2048,256]{1,0:T(8,128)(2,1)} %wq.1, f32[1,128]{1,0:T(1,128)} %bitcast.5, ...), custom_call_target="tpu_custom_call" | custom-call | tf_op jit(solution)/shard_map/layer_pass/pallas_call | solution.py:604
  79.9 2.3 %copy.11 = bf16[2048,256]{1,0:T(8,128)(2,1)} copy(bf16[2048,256]{1,0:T(8,128)(2,1)} %layer_pass.1) | data formatting | bytes 2097152

commit v5 on v4

--- a/solution.py
+++ b/solution.py
@@ -13,7 +13,8 @@
 TILE = 512
 SIDE = 4
 SPREAD_AT = 2
-SUBS = 2
+RINGED = 1
+SUBS = 4
 f32 = jnp.float32
 bf16 = jnp.bfloat16
 LEVELS = (2, 4, 8, 16, 32, 64)
@@ -85,6 +86,21 @@
     return enters, leaves, full, [link[c] * join[c] for c in range(2)]
 
 
+def upper(a, size):
+    return jnp.concatenate([a[j : j + size] for j in range(0, a.shape[0], 2 * size)], axis=0)
+
+
+def lower(a, size):
+    return jnp.concatenate([a[j + size : j + 2 * size] for j in range(0, a.shape[0], 2 * size)], axis=0)
+
+
+def spread_rows(first, second, size):
+    parts = []
+    for j in range(0, first.shape[0], size):
+        parts += [first[j : j + size], second[j : j + size]]
+    return jnp.concatenate(parts, axis=0)
+
+
 def interleave(main, side, every):
     count = 0
     for _ in main:
@@ -132,12 +148,23 @@
         a_lo[h, g] = (a - hi.astype(f32)).astype(bf16)
         xb[h, g] = pair[1] - hi * pair[0]
         yield
-    for n in range(len(LEVELS)):
-        for at_group in groups:
-            t[at_group] = dot(a_hi[at_group] * off[n], xb[at_group]).astype(bf16)
+    for n, size in enumerate(LEVELS):
+        if size < 16:
+            for k in groups:
+                t[k] = dot(a_hi[k] * off[n], xb[k]).astype(bf16)
+            yield
+            for k in groups:
+                xb[k] = xb[k] - dot(xb[k], t[k]).astype(bf16)
+            yield
+            continue
+        for k in groups:
+            low = dot(lower(a_hi[k], size) * lower(off[n], size), xb[k]).astype(bf16)
+            t[k] = spread_rows(jnp.zeros_like(low), low, size)
         yield
-        for at_group in groups:
-            xb[at_group] = xb[at_group] - dot(xb[at_group], t[at_group]).astype(bf16)
+        for k in groups:
+            low = lower(xb[k], size)
+            low = low - dot(low, t[k]).astype(bf16)
+            xb[k] = spread_rows(upper(xb[k], size), low, size)
         yield
     for h, g in groups:
         rows = slice(g * STEP, (g + 1) * STEP)
@@ -248,9 +275,10 @@
     def over(self, d, core, axis, origin):
         start = core * self.half + axis * self.wide
         block = (self.me.chips - d) * 2 + origin
+        rows = self.rows(axis) if axis < RINGED else slice(None)
         return pltpu.make_async_remote_copy(
-            src_ref=self.wo.at[self.rows(axis), start : start + self.wide],
-            dst_ref=self.w.at[block, self.rows(axis), axis * self.wide : (axis + 1) * self.wide],
+            src_ref=self.wo.at[rows, start : start + self.wide],
+            dst_ref=self.w.at[block, rows, axis * self.wide : (axis + 1) * self.wide],
             send_sem=self.over_s.at[d - 1, core, axis],
             recv_sem=self.over_r.at[d - 1, origin, axis],
             **self.me.chip(d, core),
@@ -284,10 +312,10 @@
         )
 
     def each_over(self):
-        return [(d, k, a) for d in (2, 1, 3) for k in range(2) for a in range(2)]
+        return [(d, k, a) for a in range(2) for d in (2, 1, 3) for k in range(2)]
 
     def each_ring(self):
-        return [(a, d) for d in (2, 1, 3) for a in range(2)]
+        return [(a, d) for d in (2, 1, 3) for a in range(RINGED)]
 
     def begin(self):
         for d, core, axis in self.each_over():
@@ -297,13 +325,16 @@
 
     def spread(self):
         for d, core, axis in self.each_over():
-            self.over(d, core, axis, core).wait_recv()
+            if axis < RINGED:
+                self.over(d, core, axis, core).wait_recv()
         for at in self.each_ring():
             self.ring(*at).start()
 
     def finish(self):
         for d, core, axis in self.each_over():
             self.over(d, core, axis, self.me.c).wait_send()
+            if axis >= RINGED:
+                self.over(d, core, axis, core).wait_recv()
         self.pair().wait()
         self.own().wait()
         for at in self.each_ring():
@@ -436,7 +467,7 @@
         far = lax.rem(at // 2 - self.me.y + self.me.chips, self.me.chips)
         return far, at == self.me.y * 2 + self.me.c
 
-    def run(self):
+    def run(self, weight_here):
         me, chips = self.me, self.me.chips
         order = [2, 1, 3]
         for r in range(SUBS):
@@ -448,6 +479,8 @@
                 self.share(r, d).start()
             for d in range(chips):
                 self.share(r, d).wait_recv()
+            if r == 0:
+                weight_here()
             block = self.gath[r * self.sub : (r + 1) * self.sub, :]
             w = self.w[...].reshape(self.w.shape[0] * self.w.shape[1], self.w.shape[2])
             for t in range(chips):
@@ -584,8 +617,7 @@
                     normed[rows, k * DK : (k + 1) * DK] = (o * size * out_gain[...]).astype(bf16)
                 if d:
                     mixer.there(r, d).start()
-        gather.finish()
-        mixer.run()
+        mixer.run(gather.finish)
 
 
 def layer_pass(doc, tokens, gain, wk, wv, wb, wq, out_gain, wo):

time: 82.4 us -> 79.5 us (0.965)
  Pallas kernels: 79.9 us -> 77 us
    pallas_call x1, Pallas kernels: 79.9 us -> 77 us  [layer_pass(): pl.pallas_call(layer_kernel, grid_spec=pltpu.PrefetchScalarGridSpec(num_s...]
where the time goes in v5:
time: 79.5 us; the launch traced here: 79.3 us
  Pallas kernels  77 us (97%)
  local copies, waits for them, and re-layouts  2.26 us (3%)
    pallas_call x1, Pallas kernels, layer_pass(): pl.pallas_call(layer_kernel, grid_spec=pltpu.PrefetchScalarGridSpec(num_s...  77 us
    unnamed x1, local copies, waits for them, and re-layouts  2.26 us

profile of v5, /device:TPU:1, one launch (start us, length us, event | category | flops | bytes accessed | tf_op | source)
XLA Modules:
  0.0 79.3 jit_solution(17372881510854578413)
XLA Ops:
  0.0 77.0 %layer_pass.1 = bf16[2048,256]{1,0:T(8,128)(2,1)} custom-call(s32[32]{0:T(128)} %doc.1, bf16[2048,2048]{1,0:T(8,128)(2,1)} %x.1, f32[1,2048]{1,0:T(1,128)} %bitcast.3, bf16[2048,256]{1,0:T(8,128)(2,1)} %wk.1, bf16[2048,256]{1,0:T(8,128)(2,1)} %wv.1, bf16[2,2048]{1,0:T(2,128)(2,1)} %bitcast.4, bf16[2048,256]{1,0:T(8,128)(2,1)} %wq.1, f32[1,128]{1,0:T(1,128)} %bitcast.5, ...), custom_call_target="tpu_custom_call" | custom-call | tf_op jit(solution)/shard_map/layer_pass/pallas_call | solution.py:636
  77.0 2.3 %copy.11 = bf16[2048,256]{1,0:T(8,128)(2,1)} copy(bf16[2048,256]{1,0:T(8,128)(2,1)} %layer_pass.1) | data formatting | bytes 2097152

commit v6 on v5

--- a/solution.py
+++ b/solution.py
@@ -361,7 +361,7 @@
         )
 
     def first_round(self):
-        return [self.move(self.own, self.near.at[0], 0, 1), self.move(self.own, self.near.at[1], 1, 2)]
+        return [self.move(self.own, self.near.at[1], 1, 2), self.move(self.own, self.near.at[0], 0, 1)]
 
     def second_round(self):
         return [
@@ -608,8 +608,8 @@
     @pl.when(i == 2 * tiles)
     def _():
         entering = states.entering()
-        for r in range(SUBS):
-            for d in (2, 1, 3, 0):
+        turns = [(r, d) for r in range(SUBS) for d in (2, 1, 3)]
+        for r, d in turns + [(r, 0) for r in range(SUBS)]:
                 rows = mixer.rows(d, r)
                 for k in range(len(entering)):
                     o = out[k, rows, :] + dot(carried[k, rows, :], entering[k])

time: 79.5 us -> 79.2 us (level)
  no operation moved by 1% of the time
where the time goes in v6:
time: 79.2 us; the launch traced here: 79 us
  Pallas kernels  76.7 us (97%)
  local copies, waits for them, and re-layouts  2.26 us (3%)
    pallas_call x1, Pallas kernels, layer_pass(): pl.pallas_call(layer_kernel, grid_spec=pltpu.PrefetchScalarGridSpec(num_s...  76.7 us
    unnamed x1, local copies, waits for them, and re-layouts  2.26 us

profile of v6, /device:TPU:1, one launch (start us, length us, event | category | flops | bytes accessed | tf_op | source)
XLA Modules:
  0.0 79.0 jit_solution(3766346809322274711)
XLA Ops:
  0.0 76.7 %layer_pass.1 = bf16[2048,256]{1,0:T(8,128)(2,1)} custom-call(s32[32]{0:T(128)} %doc.1, bf16[2048,2048]{1,0:T(8,128)(2,1)} %x.1, f32[1,2048]{1,0:T(1,128)} %bitcast.3, bf16[2048,256]{1,0:T(8,128)(2,1)} %wk.1, bf16[2048,256]{1,0:T(8,128)(2,1)} %wv.1, bf16[2,2048]{1,0:T(2,128)(2,1)} %bitcast.4, bf16[2048,256]{1,0:T(8,128)(2,1)} %wq.1, f32[1,128]{1,0:T(1,128)} %bitcast.5, ...), custom_call_target="tpu_custom_call" | custom-call | tf_op jit(solution)/shard_map/layer_pass/pallas_call | solution.py:636
  76.7 2.3 %copy.11 = bf16[2048,256]{1,0:T(8,128)(2,1)} copy(bf16[2048,256]{1,0:T(8,128)(2,1)} %layer_pass.1) | data formatting | bytes 2097152
